TPU v7x, 128 devices: a whole 4x4x4 slice. The times are simulated.
128 devices in a mesh: ep: 64 (over z, y, x), dp: 2 (over core).
Axes of the slice: x: 4, y: 4, z: 4, core: 2. Of those that a mesh axis runs over, the one named last changes fastest.
Arguments:
- residual: bfloat16 [9216, 2048], P(('ep', 'dp')), may hold values from -6 to 6
- queries: bfloat16 [9216, 4096], P('ep', 'dp'), may hold values from -4.5 to 4.5
- fresh_rotated_keys: bfloat16 [9216, 512], P('ep', 'dp'), may hold values from -6 to 6
- fresh_values: bfloat16 [9216, 512], P('ep', 'dp'), may hold values from -6 to 6
- cache_keys: bfloat16 [1088, 256, 512], P('ep', None, 'dp'), may hold values from -4.5 to 4.5
- request_value_cache: bfloat16 [1088, 256, 512], P('ep', None, 'dp'), may hold values from -6 to 6
- cache_lengths: int32 [1088], P('ep'), may hold values from 2 to 256, as said below
- out_proj: bfloat16 [4096, 2048], P('dp'), may hold values from -0.09375 to 0.09375
- router_weight: bfloat16 [2048, 128], replicated, may hold values from -0.125 to 0.125
- norm_gain: bfloat16 [2048], replicated, may hold values from 0.099609375 to 1.8984375
- expert_ids: int32 [9216, 8], P(('ep', 'dp')), may hold values from 0 to 127, all different within a row; in each aligned block of 72 rows (0 to 71, 72 to 143, ...) at most 9 rows name the same one
- live_mask: int32 [9216], P(('ep', 'dp')), may hold values from 0 to 1, as said below
- w_gate: bfloat16 [128, 2048, 768], P(('ep', 'dp')), may hold values from -0.125 to 0.125
- w_up: bfloat16 [128, 2048, 768], P(('ep', 'dp')), may hold values from -0.125 to 0.125
- w_down: bfloat16 [128, 768, 2048], P(('ep', 'dp')), may hold values from -0.21875 to 0.21875
Outputs:
- layer_out: bfloat16 [9216, 2048], P(('ep', 'dp'))
Inputs may be any that keep to these rules, and one draw needn't show every extreme that they name: `expert_ids`: in each aligned block of 72 rows (the rows of one device) no expert is named by more than 9 rows. `cache_lengths`: some request has exactly 256 filled slots. `live_mask`: the first 128 rows of a group are all live or all 0.
All inputs are finite; a program needn't handle non-finite values.
Results may differ from a plain program's by a relative error of at most 0.004.
Values may be sent and summed in bfloat16 or wider, within the bound.
No kernel may reach another device: no remote copies, remote signals or barrier semaphores. Data moves between devices by JAX's collectives and lax.ppermute only.
A program may use at most 128 MiB of HBM per device.

v0:
```python
import math

import jax
import jax.numpy as jnp
from jax import lax
from jax.experimental import pallas as pl
from jax.experimental.pallas import tpu as pltpu
from jax.sharding import PartitionSpec as P

HEAD = 128
NEG_FILL = -1e30
NORM_EPS = 1e-06
F32 = jnp.float32
BF16 = jnp.bfloat16
VMEM = pltpu.VMEM
LIMIT = 60 * 1024 * 1024


def dot(a, b):
    return jnp.dot(a, b, preferred_element_type=F32)


def dot_nt(a, b):
    return lax.dot_general(a, b, (((1,), (1,)), ((), ())), preferred_element_type=F32)


def dot_tn(a, b):
    return lax.dot_general(a, b, (((0,), (0,)), ((), ())), preferred_element_type=F32)


def iota(shape, axis):
    return lax.broadcasted_iota(jnp.int32, shape, axis)


def softmax_parts(scores):
    top = jnp.max(scores, -1, keepdims=True)
    raised = jnp.exp(scores - top)
    return raised, jnp.sum(raised, -1, keepdims=True)


def attend_kernel(
    lens_ref, core_ref, q_ref, fk_ref, fv_ref, ck_hbm, cv_hbm, wo_hbm,
    mine_ref, other_ref,
    k_buf, v_buf, wo_buf, att, acc, dq, dk, dv, ds, do, sem,
):
    rows, width = q_ref.shape
    requests, slots, kvw = k_buf.shape
    decode = requests - 1
    span = rows - decode
    kvh = kvw // HEAD
    heads = width // HEAD
    per = heads // kvh
    scale = 1.0 / math.sqrt(HEAD)
    half = requests // 2 + 1

    cuts = ((0, 1), (1, half), (half, requests))
    copies = []
    for i, (lo, hi) in enumerate(cuts):
        copies.append(pltpu.make_async_copy(ck_hbm.at[pl.ds(lo, hi - lo)], k_buf.at[pl.ds(lo, hi - lo)], sem.at[0, i]))
        copies.append(pltpu.make_async_copy(cv_hbm.at[pl.ds(lo, hi - lo)], v_buf.at[pl.ds(lo, hi - lo)], sem.at[1, i]))
    pieces = 4
    step = wo_buf.shape[0] // pieces
    weights = [
        pltpu.make_async_copy(wo_hbm.at[pl.ds(i * step, step)], wo_buf.at[pl.ds(i * step, step)], sem.at[2, i])
        for i in range(pieces)
    ]
    for c in copies + weights:
        c.start()

    tail = q_ref[span:, :].astype(F32)
    tail_k = fk_ref[span:, :].astype(F32)
    tail_v = fv_ref[span:, :].astype(F32)
    for h in range(heads):
        g = h // per
        dq[pl.ds(h, decode, stride=heads), :] = tail[:, h * HEAD : (h + 1) * HEAD]
        dk[pl.ds(h, decode, stride=heads), :] = tail_k[:, g * HEAD : (g + 1) * HEAD]
        dv[pl.ds(h, decode, stride=heads), :] = tail_v[:, g * HEAD : (g + 1) * HEAD]

    copies[0].wait()
    copies[1].wait()
    total = slots + span
    shape = (per * span, total)
    col = iota(shape, 1)
    place = iota(shape, 0) & (span - 1)
    allowed = ((col < slots) & (col < lens_ref[0])) | ((col >= slots) & (col - slots <= place))
    for g in range(kvh):
        gs = slice(g * HEAD, (g + 1) * HEAD)
        q = jnp.concatenate(
            [q_ref[:span, (g * per + j) * HEAD : (g * per + j + 1) * HEAD] for j in range(per)], 0
        )
        k = jnp.concatenate([k_buf[0, :, gs], fk_ref[:span, gs]], 0)
        v = jnp.concatenate([v_buf[0, :, gs], fv_ref[:span, gs]], 0)
        s = jnp.where(allowed, dot_nt(q, k) * scale, NEG_FILL)
        raised, norm = softmax_parts(s)
        p = (raised * (1.0 / norm)).astype(BF16)
        o = dot(p, v).astype(BF16)
        for j in range(per):
            h = g * per + j
            att[:span, h * HEAD : (h + 1) * HEAD] = o[j * span : (j + 1) * span]

    pairs = decode * heads
    lower = (iota((pairs, HEAD), 0) & (heads - 1)) < per
    qv = dq[...]
    qbd = jnp.concatenate([jnp.where(lower, qv, 0.0), jnp.where(lower, 0.0, qv)], 1).astype(BF16)
    own = jnp.sum(qv * dk[...], -1, keepdims=True) * scale
    lane = iota((heads, slots), 1)
    for r in range(decode):
        if r == 0:
            copies[2].wait()
        if r + 1 == half:
            copies[4].wait()
        s = dot_nt(qbd[r * heads : (r + 1) * heads], k_buf[r + 1]) * scale
        ds[r * heads : (r + 1) * heads, :] = jnp.where(lane < lens_ref[r + 1], s, NEG_FILL)
    s = ds[...]
    top = jnp.maximum(jnp.max(s, -1, keepdims=True), own)
    raised = jnp.exp(s - top)
    own_raised = jnp.exp(own - top)
    inv = 1.0 / (jnp.sum(raised, -1, keepdims=True) + own_raised)
    p = (raised * inv).astype(BF16)
    own_p = (own_raised * inv).astype(BF16).astype(F32)
    copies[3].wait()
    copies[5].wait()
    for r in range(decode):
        o = dot(p[r * heads : (r + 1) * heads], v_buf[r + 1])
        do[r * heads : r * heads + per, :] = o[:per, :HEAD]
        do[r * heads + per : (r + 1) * heads, :] = o[per:, HEAD:]
    do[...] = do[...] + own_p * dv[...]
    for h in range(heads):
        att[span:, h * HEAD : (h + 1) * HEAD] = do[pl.ds(h, decode, stride=heads), :].astype(BF16)

    for i in range(pieces):
        weights[i].wait()
    cols = wo_buf.shape[1]
    block = cols // 4
    a = att[...]
    for n in range(4):
        acc[:, n * block : (n + 1) * block] = dot(a, wo_buf[:, n * block : (n + 1) * block])
    own_rows = mine_ref.shape[0]
    core = core_ref[0]
    first = pl.multiple_of(core * own_rows, 8)
    second = pl.multiple_of((1 - core) * own_rows, 8)
    mine_ref[...] = acc[pl.ds(first, own_rows), :]
    other_ref[...] = acc[pl.ds(second, own_rows), :]


def attend(lens, core, q, fk, fv, ck, cv, wo):
    rows, width = q.shape
    requests, slots, kvw = ck.shape
    heads = width // HEAD
    pairs = (requests - 1) * heads
    own = rows // 2
    vm = pl.BlockSpec(memory_space=VMEM)
    sm = pl.BlockSpec(memory_space=pltpu.SMEM)
    hb = pl.BlockSpec(memory_space=pl.ANY)
    out = jax.ShapeDtypeStruct((own, wo.shape[1]), F32)
    return pl.pallas_call(
        attend_kernel,
        name="attend",
        out_shape=(out, out),
        in_specs=[sm, sm, vm, vm, vm, hb, hb, hb],
        out_specs=(vm, vm),
        scratch_shapes=[
            VMEM(ck.shape, BF16),
            VMEM(cv.shape, BF16),
            VMEM(wo.shape, BF16),
            VMEM((rows, width), BF16),
            VMEM((rows, wo.shape[1]), F32),
            VMEM((pairs, HEAD), F32),
            VMEM((pairs, HEAD), F32),
            VMEM((pairs, HEAD), F32),
            VMEM((pairs, slots), F32),
            VMEM((pairs, HEAD), F32),
            pltpu.SemaphoreType.DMA((3, 4)),
        ],
        compiler_params=pltpu.CompilerParams(vmem_limit_bytes=LIMIT),
    )(lens, core, q, fk, fv, ck, cv, wo)


MAIN = 8


def spread_last(scr, rows):
    tiles = scr.shape[0]
    for q in range(MAIN):
        for j in range(tiles):
            at = (q * tiles + j) * HEAD
            scr[j, pl.ds(q, rows.shape[0], stride=MAIN), :] = rows[:, at : at + HEAD]
    return jnp.concatenate([scr[j] for j in range(tiles)], 1).astype(BF16)


def collect_last(scr, pieces, count):
    tiles = scr.shape[0]
    pieces = pieces.astype(F32)
    for j in range(tiles):
        scr[j] = pieces[:, j * HEAD : (j + 1) * HEAD]
    rows = [scr[j, pl.ds(q, count, stride=MAIN), :] for q in range(MAIN) for j in range(tiles)]
    return jnp.concatenate(rows, 1).astype(BF16)


def last_scratch(rows, width):
    return VMEM((width // MAIN // HEAD, rows, HEAD), F32)


def expander(experts):
    shape = (experts, experts * MAIN)
    return ((iota(shape, 1) >> 3) == iota(shape, 0)).astype(F32).astype(BF16)


def route_kernel(
    res_ref, mine_ref, recv_ref, router_ref, gain_ref, ids_ref, live_ref,
    hidden_ref, gate_ref, rank_ref, send_ref, scr,
):
    rows, width = res_ref.shape
    experts = router_ref.shape[1]
    hidden = (res_ref[...].astype(F32) + (mine_ref[...] + recv_ref[...])).astype(BF16)
    hidden_ref[...] = hidden
    h32 = hidden.astype(F32)
    mean = jnp.mean(h32 * h32, -1, keepdims=True)
    normed = (h32 * lax.rsqrt(mean + NORM_EPS) * gain_ref[...].astype(F32)).astype(BF16)
    logits = dot(normed, router_ref[...])
    lane = iota((rows, experts), 1)
    ids = ids_ref[...]
    chosen = ids[:, 0:1] == lane
    for k in range(1, ids.shape[1]):
        chosen = chosen | (ids[:, k : k + 1] == lane)
    raised = jnp.where(chosen, jnp.exp(jnp.where(chosen, logits, 0.0)), 0.0)
    gate_ref[...] = raised / jnp.sum(raised, -1, keepdims=True)
    used = jnp.where(chosen & (live_ref[...] > 0), 1.0, 0.0)
    before = (iota((rows, rows), 0) > iota((rows, rows), 1)).astype(F32).astype(BF16)
    rank = used * (dot(before, used.astype(BF16)) + 1.0)
    rank_ref[...] = rank
    spread = dot(rank.astype(BF16), expander(experts))
    slot = (iota(spread.shape, 1) & (MAIN - 1)).astype(F32) + 1.0
    pick = jnp.where(spread == slot, 1.0, 0.0).astype(BF16)
    block = width // 4
    for n in range(4):
        cs = slice(n * block, (n + 1) * block)
        send_ref[:, cs] = dot_tn(pick, normed[:, cs]).astype(BF16)
    last = jnp.where(rank == MAIN + 1.0, 1.0, 0.0).astype(BF16)
    send_ref[:, width:] = spread_last(scr, dot_tn(last, normed))


def route(res, mine, recv, router, gain, ids, live):
    rows, width = res.shape
    experts = router.shape[1]
    part = width // MAIN
    vm = pl.BlockSpec(memory_space=VMEM)
    return pl.pallas_call(
        route_kernel,
        name="route",
        out_shape=(
            jax.ShapeDtypeStruct((rows, width), BF16),
            jax.ShapeDtypeStruct((rows, experts), F32),
            jax.ShapeDtypeStruct((rows, experts), F32),
            jax.ShapeDtypeStruct((experts * MAIN, width + part), BF16),
        ),
        in_specs=[vm] * 7,
        out_specs=(vm,) * 4,
        scratch_shapes=[last_scratch(experts * MAIN, width)],
        compiler_params=pltpu.CompilerParams(vmem_limit_bytes=LIMIT),
    )(res, mine, recv, router, gain, ids, live)


def expert_kernel(x_ref, wg_hbm, wu_hbm, wd_hbm, y_ref, wg, wu, wd, scr, sem):
    width = wg.shape[0]
    copies = [
        pltpu.make_async_copy(wg_hbm.at[0], wg, sem.at[0]),
        pltpu.make_async_copy(wu_hbm.at[0], wu, sem.at[1]),
        pltpu.make_async_copy(wd_hbm.at[0], wd, sem.at[2]),
    ]
    for c in copies:
        c.start()

    def mlp(x):
        g = dot(x, wg[...])
        u = dot(x, wu[...])
        return dot((g * jax.nn.sigmoid(g) * u).astype(BF16), wd[...])

    count = x_ref.shape[0]
    last = collect_last(scr, x_ref[:, width:], count // MAIN)
    for c in copies:
        c.wait()
    y_ref[:, width:] = spread_last(scr, mlp(last))
    chunk = 256

    @pl.loop(0, count // chunk)
    def _(i):
        rows = pl.ds(pl.multiple_of(i * chunk, chunk), chunk)
        y_ref[rows, :width] = mlp(x_ref[rows, :width]).astype(BF16)


def expert(x, wg, wu, wd):
    vm = pl.BlockSpec(memory_space=VMEM)
    hb = pl.BlockSpec(memory_space=pl.ANY)
    return pl.pallas_call(
        expert_kernel,
        name="expert",
        out_shape=jax.ShapeDtypeStruct(x.shape, BF16),
        in_specs=[vm, hb, hb, hb],
        out_specs=vm,
        scratch_shapes=[
            VMEM(wg.shape[1:], BF16),
            VMEM(wu.shape[1:], BF16),
            VMEM(wd.shape[1:], BF16),
            last_scratch(x.shape[0], wg.shape[1]),
            pltpu.SemaphoreType.DMA((3,)),
        ],
        compiler_params=pltpu.CompilerParams(vmem_limit_bytes=LIMIT),
    )(x, wg, wu, wd)


def combine_kernel(hidden_ref, gate_ref, rank_ref, y_ref, out_ref, scr):
    rows, width = hidden_ref.shape
    experts = gate_ref.shape[1]
    rank = rank_ref[...]
    gate = gate_ref[...]
    high = gate.astype(BF16).astype(F32)
    both = jnp.concatenate([high, gate - high], 0)
    rank2 = jnp.concatenate([rank, rank], 0)
    grow = expander(experts)
    spread = dot(rank2.astype(BF16), grow)
    slot = (iota(spread.shape, 1) & (MAIN - 1)).astype(F32) + 1.0
    main = jnp.where(spread == slot, dot(both.astype(BF16), grow), 0.0).astype(BF16)
    last = jnp.where(rank2 == MAIN + 1.0, both, 0.0).astype(BF16)
    tail = collect_last(scr, y_ref[:, width:], experts)
    block = width // 4
    for n in range(4):
        cs = slice(n * block, (n + 1) * block)
        mix = dot(main, y_ref[:, cs]) + dot(last, tail[:, cs])
        out_ref[:, cs] = (hidden_ref[:, cs].astype(F32) + (mix[:rows] + mix[rows:])).astype(BF16)


def combine(hidden, gate, rank, y):
    vm = pl.BlockSpec(memory_space=VMEM)
    return pl.pallas_call(
        combine_kernel,
        name="combine",
        out_shape=jax.ShapeDtypeStruct(hidden.shape, BF16),
        in_specs=[vm] * 4,
        out_specs=vm,
        scratch_shapes=[last_scratch(y.shape[0], hidden.shape[1])],
        compiler_params=pltpu.CompilerParams(vmem_limit_bytes=LIMIT),
    )(hidden, gate, rank, y)


def exchange(x, experts):
    blocks = x.reshape(experts, MAIN, x.shape[1])
    moved = lax.all_to_all(blocks, ("ep", "dp"), split_axis=0, concat_axis=0, tiled=True)
    return moved.reshape(x.shape)


def on_device(
    residual, queries, fresh_rotated_keys, fresh_values, cache_keys, request_value_cache,
    cache_lengths, out_proj, router_weight, norm_gain, expert_ids, live_mask,
    w_gate, w_up, w_down,
):
    experts = router_weight.shape[1]
    core = lax.axis_index("dp").astype(jnp.int32).reshape(1)
    mine, other = attend(
        cache_lengths, core, queries, fresh_rotated_keys, fresh_values, cache_keys,
        request_value_cache, out_proj,
    )
    recv = lax.ppermute(other, "dp", [(0, 1), (1, 0)])
    hidden, gate, rank, send = route(
        residual, mine, recv, router_weight, norm_gain.reshape(1, -1), expert_ids,
        live_mask.reshape(-1, 1),
    )
    back = exchange(expert(exchange(send, experts), w_gate, w_up, w_down), experts)
    return combine(hidden, gate, rank, back)


def solution(mesh):
    both = ("ep", "dp")
    placed = (
        P(both, None),
        P("ep", "dp"),
        P("ep", "dp"),
        P("ep", "dp"),
        P("ep", None, "dp"),
        P("ep", None, "dp"),
        P("ep"),
        P("dp", None),
        P(),
        P(),
        P(both, None),
        P(both),
        P(both, None, None),
        P(both, None, None),
        P(both, None, None),
    )
    return jax.shard_map(
        on_device, mesh=mesh, in_specs=placed, out_specs=P(both, None), check_vma=False
    )
```

profile of v0, /device:TPU:1, one launch (start us, length us, event | category | flops | bytes accessed | tf_op | source)
XLA Modules:
  0.0 176.5 jit_solution(3959501896539617331)
XLA Ops:
  0.0 0.0 copy-start.1
  0.0 0.0 copy-start.2
  0.0 0.0 copy-start.3
  0.0 8.5 %attend.1 = (f32[72,2048]{1,0:T(8,128)}, f32[72,2048]{1,0:T(8,128)}) custom-call(s32[17]{0:T(128)} %lens_ref.1, s32[1]{0:T(128)} %bitcast.core_ref, bf16[144,2048]{1,0:T(8,128)(2,1)} %q_ref.1, bf16[144,256]{1,0:T(8,128)(2,1)} %fk_ref.1, bf16[144,256]{1,0:T(8,128)(2,1)} %fv_ref.1, bf16[17,256,256]{2,1,0:T(8,128)(2,1)} %ck_hbm.1, ...), custom_call_target="tpu_custom_call" | custom-call | tf_op jit(solution)/shard_map/attend/pallas_call | solution.py:156
  8.5 1.5 collective-permute-start
  10.0 0.0 copy-done.1
  10.0 0.6 reshape.22.gain_ref
  10.6 0.0 copy-done.2
  10.6 0.7 copy.16.ids_ref
  11.3 0.0 copy-done.3
  11.3 0.7 copy.17.live_ref
  12.0 0.0 collective-permute-done.recv_ref
  12.0 0.0 copy-start
  12.0 0.9 copy-done
  12.9 5.8 %route.1 = (bf16[72,2048]{1,0:T(8,128)(2,1)}, f32[72,128]{1,0:T(8,128)}, f32[72,128]{1,0:T(8,128)}, bf16[1024,2304]{1,0:T(8,128)(2,1)}) custom-call(bf16[72,2048]{1,0:T(8,128)(2,1)} %res_ref.1, f32[72,2048]{1,0:T(8,128)} %get-tuple-element.11.mine_ref, f32[72,2048]{1,0:T(8,128)} %copy-done, bf16[2048,128]{1,0:T(8,128)(2,1)} %router_ref.1, ...), custom_call_target="tpu_custom_call" | custom-call | tf_op jit(solution)/shard_map/route/pallas_call | solution.py:248
  18.7 69.0 %all_to_all.10 = bf16[128,8,2304]{2,1,0:T(8,128)(2,1)} all-to-all(bf16[128,8,2304]{2,1,0:T(8,128)(2,1)} %bitcast.9), channel_id=1, replica_groups=mesh['ep'=64,'dp'=2] {'ep','dp'}, dimensions={0} | all-to-all | bytes 9437184 | tf_op jit(solution)/shard_map/all_to_all | solution.py:348
  87.7 20.3 %expert.1 = bf16[1024,2304]{1,0:T(8,128)(2,1)} custom-call(bf16[1024,2304]{1,0:T(8,128)(2,1)} %bitcast.7, bf16[1,2048,768]{2,1,0:T(8,128)(2,1)} %wg_hbm.1, bf16[1,2048,768]{2,1,0:T(8,128)(2,1)} %wu_hbm.1, bf16[1,768,2048]{2,1,0:T(8,128)(2,1)} %wd_hbm.1), custom_call_target="tpu_custom_call" | custom-call | tf_op jit(solution)/shard_map/expert/pallas_call | solution.py:295
  108.0 64.1 %all_to_all.11 = bf16[128,8,2304]{2,1,0:T(8,128)(2,1)} all-to-all(bf16[128,8,2304]{2,1,0:T(8,128)(2,1)} %bitcast.8), channel_id=1, replica_groups=mesh['ep'=64,'dp'=2] {'ep','dp'}, dimensions={0} | all-to-all | bytes 9437184 | tf_op jit(solution)/shard_map/all_to_all | solution.py:348
  172.1 4.4 %combine.1 = bf16[72,2048]{1,0:T(8,128)(2,1)} custom-call(bf16[72,2048]{1,0:T(8,128)(2,1)} %get-tuple-element.13.hidden_ref, f32[72,128]{1,0:T(8,128)} %get-tuple-element.14.gate_ref, f32[72,128]{1,0:T(8,128)} %get-tuple-element.15.rank_ref, bf16[1024,2304]{1,0:T(8,128)(2,1)} %bitcast.6), custom_call_target="tpu_custom_call" | custom-call | tf_op jit(solution)/shard_map/combine/pallas_call | solution.py:335
Async XLA Ops:
  0.0 10.0 %copy-start.1 = (bf16[2048]{0:T(1024)(128)(2,1)S(1)}, bf16[2048]{0:T(1024)(128)(2,1)}, u32[]{:S(2)}) copy-start(bf16[2048]{0:T(1024)(128)(2,1)} %param.24) | copy-start | bytes 12292
  0.0 10.6 %copy-start.2 = (s32[72,8]{0,1:T(8,128)S(1)}, s32[72,8]{0,1:T(8,128)}, u32[]{:S(2)}) copy-start(s32[72,8]{0,1:T(8,128)} %param.25) | copy-start | bytes 6916
  0.0 11.3 %copy-start.3 = (s32[72]{0:T(128)S(1)}, s32[72]{0:T(128)}, u32[]{:S(2)}) copy-start(s32[72]{0:T(128)} %param.26) | copy-start | bytes 868
  8.5 3.5 %collective-permute-start = (f32[72,2048]{1,0:T(8,128)}, f32[72,2048]{1,0:T(8,128)S(1)}, u32[]{:S(2)}, u32[]{:S(2)}) collective-permute-start(f32[72,2048]{1,0:T(8,128)} %get-tuple-element.12), channel_id=1, source_target_pairs={{0,1},{1,0},{2,3},{3,2},{4,5},{5,4},{6,7},{7,6},{8,9},{9,8},{10,11... | collective-permute-start | bytes 1769480 | tf_op jit(solution)/shard_map/ppermute | solution.py:363
  12.0 0.9 copy-start
where the time goes:
time: 177 us
  blocking collectives  133 us (75%)
  Pallas kernels  39.1 us (22%)
  local copies, waits for them, and re-layouts  2.88 us (2%)
    all_to_all x2, blocking collectives, exchange(): lax.all_to_all(blocks, ('ep', 'dp'), split_axis=0, concat_axis=0, tiled=T...  133 us
    pallas_call x1, Pallas kernels, expert(): pl.pallas_call(expert_kernel, name='expert', out_shape=jax.ShapeDtypeStru...  20.3 us
    pallas_call x1, Pallas kernels, attend(): pl.pallas_call(attend_kernel, name='attend', out_shape=(out, out), in_spe...  8.53 us
    pallas_call x1, Pallas kernels, route(): pl.pallas_call(route_kernel, name='route', out_shape=(jax.ShapeDtypeStruc...  5.82 us
    pallas_call x1, Pallas kernels, combine(): pl.pallas_call(combine_kernel, name='combine', out_shape=jax.ShapeDtypeSt...  4.39 us
  transfers between devices with their start and end apart: 1, of which 0 were waited for; matrix products, arithmetic and copies ran while one was open for 1% of the time, Pallas kernels for 0%

commit v1 on v0

--- a/solution.py
+++ b/solution.py
@@ -13,7 +13,8 @@
 F32 = jnp.float32
 BF16 = jnp.bfloat16
 VMEM = pltpu.VMEM
-LIMIT = 60 * 1024 * 1024
+LIMIT = 30 * 1024 * 1024
+FULL = 60 * 1024 * 1024
 
 
 def dot(a, b):
@@ -39,9 +40,9 @@
 
 
 def attend_kernel(
-    lens_ref, core_ref, q_ref, fk_ref, fv_ref, ck_hbm, cv_hbm, wo_hbm,
+    lens_ref, core_ref, q_hbm, fk_hbm, fv_hbm, ck_hbm, cv_hbm, wo_hbm,
     mine_ref, other_ref,
-    k_buf, v_buf, wo_buf, att, acc, dq, dk, dv, ds, do, sem,
+    q_ref, fk_ref, fv_ref, k_buf, v_buf, wo_buf, att, acc, dq, dk, dv, ds, do, sem,
 ):
     rows, width = q_ref.shape
     requests, slots, kvw = k_buf.shape
@@ -64,8 +65,14 @@
         pltpu.make_async_copy(wo_hbm.at[pl.ds(i * step, step)], wo_buf.at[pl.ds(i * step, step)], sem.at[2, i])
         for i in range(pieces)
     ]
-    for c in copies + weights:
+    small = [
+        pltpu.make_async_copy(src, dst, sem.at[3, i])
+        for i, (src, dst) in enumerate(((q_hbm, q_ref), (fk_hbm, fk_ref), (fv_hbm, fv_ref)))
+    ]
+    for c in small + copies + weights:
         c.start()
+    for c in small:
+        c.wait()
 
     tail = q_ref[span:, :].astype(F32)
     tail_k = fk_ref[span:, :].astype(F32)
@@ -157,9 +164,12 @@
         attend_kernel,
         name="attend",
         out_shape=(out, out),
-        in_specs=[sm, sm, vm, vm, vm, hb, hb, hb],
+        in_specs=[sm, sm] + [hb] * 6,
         out_specs=(vm, vm),
         scratch_shapes=[
+            VMEM(q.shape, BF16),
+            VMEM(fk.shape, BF16),
+            VMEM(fv.shape, BF16),
             VMEM(ck.shape, BF16),
             VMEM(cv.shape, BF16),
             VMEM(wo.shape, BF16),
@@ -170,9 +180,9 @@
             VMEM((pairs, HEAD), F32),
             VMEM((pairs, slots), F32),
             VMEM((pairs, HEAD), F32),
-            pltpu.SemaphoreType.DMA((3, 4)),
+            pltpu.SemaphoreType.DMA((4, 4)),
         ],
-        compiler_params=pltpu.CompilerParams(vmem_limit_bytes=LIMIT),
+        compiler_params=pltpu.CompilerParams(vmem_limit_bytes=FULL),
     )(lens, core, q, fk, fv, ck, cv, wo)
 
 
@@ -261,15 +271,9 @@
     )(res, mine, recv, router, gain, ids, live)
 
 
-def expert_kernel(x_ref, wg_hbm, wu_hbm, wd_hbm, y_ref, wg, wu, wd, scr, sem):
+def expert_kernel(x_ref, wg_ref, wu_ref, wd_ref, y_ref, scr):
+    wg, wu, wd = wg_ref.at[0], wu_ref.at[0], wd_ref.at[0]
     width = wg.shape[0]
-    copies = [
-        pltpu.make_async_copy(wg_hbm.at[0], wg, sem.at[0]),
-        pltpu.make_async_copy(wu_hbm.at[0], wu, sem.at[1]),
-        pltpu.make_async_copy(wd_hbm.at[0], wd, sem.at[2]),
-    ]
-    for c in copies:
-        c.start()
 
     def mlp(x):
         g = dot(x, wg[...])
@@ -278,8 +282,6 @@
 
     count = x_ref.shape[0]
     last = collect_last(scr, x_ref[:, width:], count // MAIN)
-    for c in copies:
-        c.wait()
     y_ref[:, width:] = spread_last(scr, mlp(last))
     chunk = 256
 
@@ -291,20 +293,13 @@
 
 def expert(x, wg, wu, wd):
     vm = pl.BlockSpec(memory_space=VMEM)
-    hb = pl.BlockSpec(memory_space=pl.ANY)
     return pl.pallas_call(
         expert_kernel,
         name="expert",
         out_shape=jax.ShapeDtypeStruct(x.shape, BF16),
-        in_specs=[vm, hb, hb, hb],
+        in_specs=[vm] * 4,
         out_specs=vm,
-        scratch_shapes=[
-            VMEM(wg.shape[1:], BF16),
-            VMEM(wu.shape[1:], BF16),
-            VMEM(wd.shape[1:], BF16),
-            last_scratch(x.shape[0], wg.shape[1]),
-            pltpu.SemaphoreType.DMA((3,)),
-        ],
+        scratch_shapes=[last_scratch(x.shape[0], wg.shape[1])],
         compiler_params=pltpu.CompilerParams(vmem_limit_bytes=LIMIT),
     )(x, wg, wu, wd)
 

time: 177 us -> 161 us (0.910)
  Pallas kernels: 39.1 us -> 24.6 us
    pallas_call x1, Pallas kernels: 20.3 us -> 12.1 us  [expert(): pl.pallas_call(expert_kernel, name='expert', out_shape=jax.ShapeDtypeStru...]
    pallas_call x1, Pallas kernels: 5.82 us -> 2.2 us  [route(): pl.pallas_call(route_kernel, name='route', out_shape=(jax.ShapeDtypeStruc...]
    pallas_call x1, Pallas kernels: 4.39 us -> 2 us  [combine(): pl.pallas_call(combine_kernel, name='combine', out_shape=jax.ShapeDtypeSt...]
  transfers between devices with their start and end apart: 1 -> 1, of which waited for: 0 -> 1; matrix products, arithmetic and copies ran while one was open for 1% -> 0% of each run, Pallas kernels for 0% -> 0%
where the time goes in v1:
time: 161 us
  blocking collectives  132 us (82%)
  Pallas kernels  24.6 us (15%)
  waiting for transfers between devices  1.63 us (1%)
    all_to_all x2, blocking collectives, exchange(): lax.all_to_all(blocks, ('ep', 'dp'), split_axis=0, concat_axis=0, tiled=T...  132 us
    pallas_call x1, Pallas kernels, expert(): pl.pallas_call(expert_kernel, name='expert', out_shape=jax.ShapeDtypeStru...  12.1 us
    pallas_call x1, Pallas kernels, attend(): pl.pallas_call(attend_kernel, name='attend', out_shape=(out, out), in_spe...  8.35 us
  transfers between devices with their start and end apart: 1, of which 1 were waited for; matrix products, arithmetic and copies ran while one was open for 0% of the time, Pallas kernels for 0%

profile of v1, /device:TPU:1, one launch (start us, length us, event | category | flops | bytes accessed | tf_op | source)
XLA Modules:
  0.0 160.9 jit_solution(15367157247552822069)
XLA Ops:
  0.0 0.0 copy-start.4
  0.0 0.0 copy-start.5
  0.0 8.4 %attend.1 = (f32[72,2048]{1,0:T(8,128)}, f32[72,2048]{1,0:T(8,128)}) custom-call(s32[17]{0:T(128)} %lens_ref.1, s32[1]{0:T(128)} %bitcast.core_ref, bf16[144,2048]{1,0:T(8,128)(2,1)} %q_hbm.1, bf16[144,256]{1,0:T(8,128)(2,1)} %fk_hbm.1, bf16[144,256]{1,0:T(8,128)(2,1)} %fv_hbm.1, bf16[17,256,256]{2,1,0:T(8,128)(2,1)} %ck_hbm.1, ...), custom_call_target="tpu_custom_call" | custom-call | tf_op jit(solution)/shard_map/attend/pallas_call | solution.py:163
  8.4 1.4 collective-permute-start
  9.8 0.0 copy-done.6
  9.9 0.0 copy-done.7
  9.9 0.1 copy.16.ids_ref
  10.0 0.0 copy-done.8
  10.0 0.1 copy.17.live_ref
  10.1 1.6 %collective-permute-done.recv_ref = f32[72,2048]{1,0:T(8,128)S(1)} collective-permute-done((f32[72,2048]{1,0:T(8,128)}, f32[72,2048]{1,0:T(8,128)S(1)}, u32[]{:S(2)}, u32[]{:S(2)}) %collective-permute-start) | collective-permute-done | bytes 589856 | tf_op jit(solution)/shard_map/ppermute | solution.py:358
  11.7 0.0 copy-done.4
  11.7 0.0 copy-done.5
  11.7 1.1 copy-done.3
  12.8 2.2 %route.1 = (bf16[72,2048]{1,0:T(8,128)(2,1)S(1)}, f32[72,128]{1,0:T(8,128)S(1)}, f32[72,128]{1,0:T(8,128)S(1)}, bf16[1024,2304]{1,0:T(8,128)(2,1)S(1)}) custom-call(bf16[72,2048]{1,0:T(8,128)(2,1)S(1)} %copy-done.5, f32[72,2048]{1,0:T(8,128)S(1)} %copy-done.3, f32[72,2048]{1,0:T(8,128)S(1)} %collective-permute-done.recv_ref, ...), custom_call_target="tpu_custom_call" | custom-call | tf_op jit(solution)/shard_map/route/pallas_call | solution.py:258
  15.0 0.0 copy-start
  15.0 0.0 copy-start.1
  15.0 0.0 copy-start.2
  15.0 68.8 %all_to_all.10 = bf16[128,8,2304]{2,1,0:T(8,128)(2,1)S(1)} all-to-all(bf16[128,8,2304]{2,1,0:T(8,128)(2,1)S(1)} %bitcast.9), channel_id=1, replica_groups=mesh['ep'=64,'dp'=2] {'ep','dp'}, dimensions={0} | all-to-all | bytes 9437184 | tf_op jit(solution)/shard_map/all_to_all | solution.py:343
  83.8 0.0 copy-done
  83.9 0.0 copy-done.1
  83.9 0.0 copy-done.2
  83.9 12.1 %expert.1 = bf16[1024,2304]{1,0:T(8,128)(2,1)S(1)} custom-call(bf16[1024,2304]{1,0:T(8,128)(2,1)S(1)} %bitcast.7, bf16[1,2048,768]{2,1,0:T(8,128)(2,1)S(1)} %copy-done, bf16[1,2048,768]{2,1,0:T(8,128)(2,1)S(1)} %copy-done.1, bf16[1,768,2048]{2,1,0:T(8,128)(2,1)S(1)} %copy-done.2), custom_call_target="tpu_custom_call" | custom-call | tf_op jit(solution)/shard_map/expert/pallas_call | solution.py:296
  96.0 63.0 %all_to_all.11 = bf16[128,8,2304]{2,1,0:T(8,128)(2,1)S(1)} all-to-all(bf16[128,8,2304]{2,1,0:T(8,128)(2,1)S(1)} %bitcast.8), channel_id=1, replica_groups=mesh['ep'=64,'dp'=2] {'ep','dp'}, dimensions={0} | all-to-all | bytes 9437184 | tf_op jit(solution)/shard_map/all_to_all | solution.py:343
  158.9 2.0 %combine.1 = bf16[72,2048]{1,0:T(8,128)(2,1)} custom-call(bf16[72,2048]{1,0:T(8,128)(2,1)S(1)} %get-tuple-element.13.hidden_ref, f32[72,128]{1,0:T(8,128)S(1)} %get-tuple-element.14.gate_ref, f32[72,128]{1,0:T(8,128)S(1)} %get-tuple-element.15.rank_ref, bf16[1024,2304]{1,0:T(8,128)(2,1)S(1)} %bitcast.6), custom_call_target="tpu_custom_call" | custom-call | tf_op jit(solution)/shard_map/combine/pallas_call | solution.py:330
  (5 shorter events, 0.0 us)
Async XLA Ops:
  0.0 9.8 %copy-start.6 = (bf16[2048]{0:T(1024)(128)(2,1)S(1)}, bf16[2048]{0:T(1024)(128)(2,1)}, u32[]{:S(2)}) copy-start(bf16[2048]{0:T(1024)(128)(2,1)} %param.24) | copy-start | bytes 12292
  0.0 9.9 %copy-start.7 = (s32[72,8]{0,1:T(8,128)S(1)}, s32[72,8]{0,1:T(8,128)}, u32[]{:S(2)}) copy-start(s32[72,8]{0,1:T(8,128)} %param.25) | copy-start | bytes 6916
  0.0 9.9 %copy-start.8 = (s32[72]{0:T(128)S(1)}, s32[72]{0:T(128)}, u32[]{:S(2)}) copy-start(s32[72]{0:T(128)} %param.26) | copy-start | bytes 868
  0.0 11.7 %copy-start.4 = (bf16[2048,128]{1,0:T(8,128)(2,1)S(1)}, bf16[2048,128]{1,0:T(8,128)(2,1)}, u32[]{:S(2)}) copy-start(bf16[2048,128]{1,0:T(8,128)(2,1)} %router_ref.1) | copy-start | bytes 1572868
  0.0 11.7 %copy-start.5 = (bf16[72,2048]{1,0:T(8,128)(2,1)S(1)}, bf16[72,2048]{1,0:T(8,128)(2,1)}, u32[]{:S(2)}) copy-start(bf16[72,2048]{1,0:T(8,128)(2,1)} %res_ref.1) | copy-start | bytes 884740
  8.4 3.3 %collective-permute-start = (f32[72,2048]{1,0:T(8,128)}, f32[72,2048]{1,0:T(8,128)S(1)}, u32[]{:S(2)}, u32[]{:S(2)}) collective-permute-start(f32[72,2048]{1,0:T(8,128)} %get-tuple-element.12), channel_id=1, source_target_pairs={{0,1},{1,0},{2,3},{3,2},{4,5},{5,4},{6,7},{7,6},{8,9},{9,8},{10,11... | collective-permute-start | bytes 1769480 | tf_op jit(solution)/shard_map/ppermute | solution.py:358
  11.7 1.1 copy-start.3
  15.0 68.9 %copy-start = (bf16[1,2048,768]{2,1,0:T(8,128)(2,1)S(1)}, bf16[1,2048,768]{2,1,0:T(8,128)(2,1)}, u32[]{:S(2)}) copy-start(bf16[1,2048,768]{2,1,0:T(8,128)(2,1)} %wg_ref.1) | copy-start | bytes 9437188
  15.0 68.9 %copy-start.1 = (bf16[1,2048,768]{2,1,0:T(8,128)(2,1)S(1)}, bf16[1,2048,768]{2,1,0:T(8,128)(2,1)}, u32[]{:S(2)}) copy-start(bf16[1,2048,768]{2,1,0:T(8,128)(2,1)} %wu_ref.1) | copy-start | bytes 9437188
  15.0 68.9 %copy-start.2 = (bf16[1,768,2048]{2,1,0:T(8,128)(2,1)S(1)}, bf16[1,768,2048]{2,1,0:T(8,128)(2,1)}, u32[]{:S(2)}) copy-start(bf16[1,768,2048]{2,1,0:T(8,128)(2,1)} %wd_ref.1) | copy-start | bytes 9437188

commit v2 on v1

--- a/solution.py
+++ b/solution.py
@@ -41,7 +41,7 @@
 
 def attend_kernel(
     lens_ref, core_ref, q_hbm, fk_hbm, fv_hbm, ck_hbm, cv_hbm, wo_hbm,
-    mine_ref, other_ref,
+    mine_hbm, other_hbm,
     q_ref, fk_ref, fv_ref, k_buf, v_buf, wo_buf, att, acc, dq, dk, dv, ds, do, sem,
 ):
     rows, width = q_ref.shape
@@ -60,9 +60,9 @@
         copies.append(pltpu.make_async_copy(ck_hbm.at[pl.ds(lo, hi - lo)], k_buf.at[pl.ds(lo, hi - lo)], sem.at[0, i]))
         copies.append(pltpu.make_async_copy(cv_hbm.at[pl.ds(lo, hi - lo)], v_buf.at[pl.ds(lo, hi - lo)], sem.at[1, i]))
     pieces = 4
-    step = wo_buf.shape[0] // pieces
+    step = wo_buf.shape[1] // pieces
     weights = [
-        pltpu.make_async_copy(wo_hbm.at[pl.ds(i * step, step)], wo_buf.at[pl.ds(i * step, step)], sem.at[2, i])
+        pltpu.make_async_copy(wo_hbm.at[:, pl.ds(i * step, step)], wo_buf.at[:, pl.ds(i * step, step)], sem.at[2, i])
         for i in range(pieces)
     ]
     small = [
@@ -135,19 +135,22 @@
     for h in range(heads):
         att[span:, h * HEAD : (h + 1) * HEAD] = do[pl.ds(h, decode, stride=heads), :].astype(BF16)
 
-    for i in range(pieces):
-        weights[i].wait()
-    cols = wo_buf.shape[1]
-    block = cols // 4
-    a = att[...]
-    for n in range(4):
-        acc[:, n * block : (n + 1) * block] = dot(a, wo_buf[:, n * block : (n + 1) * block])
-    own_rows = mine_ref.shape[0]
+    own_rows = mine_hbm.shape[0]
     core = core_ref[0]
     first = pl.multiple_of(core * own_rows, 8)
     second = pl.multiple_of((1 - core) * own_rows, 8)
-    mine_ref[...] = acc[pl.ds(first, own_rows), :]
-    other_ref[...] = acc[pl.ds(second, own_rows), :]
+    a = att[...]
+    leaving = []
+    for i in range(pieces):
+        weights[i].wait()
+        cs = pl.ds(i * step, step)
+        acc[:, cs] = dot(a, wo_buf[:, cs])
+        for n, (at, dst) in enumerate(((second, other_hbm), (first, mine_hbm))):
+            c = pltpu.make_async_copy(acc.at[pl.ds(at, own_rows), cs], dst.at[:, cs], sem.at[4 + n, i])
+            c.start()
+            leaving.append(c)
+    for c in leaving:
+        c.wait()
 
 
 def attend(lens, core, q, fk, fv, ck, cv, wo):
@@ -156,7 +159,6 @@
     heads = width // HEAD
     pairs = (requests - 1) * heads
     own = rows // 2
-    vm = pl.BlockSpec(memory_space=VMEM)
     sm = pl.BlockSpec(memory_space=pltpu.SMEM)
     hb = pl.BlockSpec(memory_space=pl.ANY)
     out = jax.ShapeDtypeStruct((own, wo.shape[1]), F32)
@@ -165,7 +167,7 @@
         name="attend",
         out_shape=(out, out),
         in_specs=[sm, sm] + [hb] * 6,
-        out_specs=(vm, vm),
+        out_specs=(hb, hb),
         scratch_shapes=[
             VMEM(q.shape, BF16),
             VMEM(fk.shape, BF16),
@@ -180,7 +182,7 @@
             VMEM((pairs, HEAD), F32),
             VMEM((pairs, slots), F32),
             VMEM((pairs, HEAD), F32),
-            pltpu.SemaphoreType.DMA((4, 4)),
+            pltpu.SemaphoreType.DMA((6, 4)),
         ],
         compiler_params=pltpu.CompilerParams(vmem_limit_bytes=FULL),
     )(lens, core, q, fk, fv, ck, cv, wo)
@@ -217,12 +219,12 @@
 
 
 def route_kernel(
-    res_ref, mine_ref, recv_ref, router_ref, gain_ref, ids_ref, live_ref,
+    base_ref, recv_ref, router_ref, gain_ref, ids_ref, live_ref,
     hidden_ref, gate_ref, rank_ref, send_ref, scr,
 ):
-    rows, width = res_ref.shape
+    rows, width = base_ref.shape
     experts = router_ref.shape[1]
-    hidden = (res_ref[...].astype(F32) + (mine_ref[...] + recv_ref[...])).astype(BF16)
+    hidden = (base_ref[...] + recv_ref[...]).astype(BF16)
     hidden_ref[...] = hidden
     h32 = hidden.astype(F32)
     mean = jnp.mean(h32 * h32, -1, keepdims=True)
@@ -250,8 +252,8 @@
     send_ref[:, width:] = spread_last(scr, dot_tn(last, normed))
 
 
-def route(res, mine, recv, router, gain, ids, live):
-    rows, width = res.shape
+def route(base, recv, router, gain, ids, live):
+    rows, width = base.shape
     experts = router.shape[1]
     part = width // MAIN
     vm = pl.BlockSpec(memory_space=VMEM)
@@ -264,11 +266,11 @@
             jax.ShapeDtypeStruct((rows, experts), F32),
             jax.ShapeDtypeStruct((experts * MAIN, width + part), BF16),
         ),
-        in_specs=[vm] * 7,
+        in_specs=[vm] * 6,
         out_specs=(vm,) * 4,
         scratch_shapes=[last_scratch(experts * MAIN, width)],
         compiler_params=pltpu.CompilerParams(vmem_limit_bytes=LIMIT),
-    )(res, mine, recv, router, gain, ids, live)
+    )(base, recv, router, gain, ids, live)
 
 
 def expert_kernel(x_ref, wg_ref, wu_ref, wd_ref, y_ref, scr):
@@ -357,7 +359,7 @@
     )
     recv = lax.ppermute(other, "dp", [(0, 1), (1, 0)])
     hidden, gate, rank, send = route(
-        residual, mine, recv, router_weight, norm_gain.reshape(1, -1), expert_ids,
+        residual.astype(F32) + mine, recv, router_weight, norm_gain.reshape(1, -1), expert_ids,
         live_mask.reshape(-1, 1),
     )
     back = exchange(expert(exchange(send, experts), w_gate, w_up, w_down), experts)

time: 161 us -> 160 us (level)
  transfers between devices with their start and end apart: 1 -> 1, of which waited for: 1 -> 1; matrix products, arithmetic and copies ran while one was open for 0% -> 1% of each run, Pallas kernels for 0% -> 0%
where the time goes in v2:
time: 160 us
  blocking collectives  132 us (82%)
  Pallas kernels  24.3 us (15%)
    all_to_all x2, blocking collectives, exchange(): lax.all_to_all(blocks, ('ep', 'dp'), split_axis=0, concat_axis=0, tiled=T...  132 us
    pallas_call x1, Pallas kernels, expert(): pl.pallas_call(expert_kernel, name='expert', out_shape=jax.ShapeDtypeStru...  12.1 us
    pallas_call x1, Pallas kernels, attend(): pl.pallas_call(attend_kernel, name='attend', out_shape=(out, out), in_spe...  8.11 us
  transfers between devices with their start and end apart: 1, of which 1 were waited for; matrix products, arithmetic and copies ran while one was open for 1% of the time, Pallas kernels for 0%

profile of v2, /device:TPU:1, one launch (start us, length us, event | category | flops | bytes accessed | tf_op | source)
XLA Modules:
  0.0 159.5 jit_solution(16854277068374838345)
XLA Ops:
  0.0 0.0 copy-start.4
  0.0 0.0 copy-start.3
  0.0 8.1 %attend.1 = (f32[72,2048]{1,0:T(8,128)}, f32[72,2048]{1,0:T(8,128)}) custom-call(s32[17]{0:T(128)} %lens_ref.1, s32[1]{0:T(128)} %bitcast.core_ref, bf16[144,2048]{1,0:T(8,128)(2,1)} %q_hbm.1, bf16[144,256]{1,0:T(8,128)(2,1)} %fk_hbm.1, bf16[144,256]{1,0:T(8,128)(2,1)} %fv_hbm.1, bf16[17,256,256]{2,1,0:T(8,128)(2,1)} %ck_hbm.1, ...), custom_call_target="tpu_custom_call" | custom-call | tf_op jit(solution)/shard_map/attend/pallas_call | solution.py:165
  8.2 1.5 collective-permute-start
  9.6 0.0 copy-done.5
  9.6 0.0 copy-done.6
  9.6 0.1 copy.16.ids_ref
  9.7 0.0 copy-done.7
  9.7 0.1 copy.17.live_ref
  9.8 0.0 copy-done.4
  9.8 1.1 convert_add_fusion.base_ref
  10.9 0.5 collective-permute-done.recv_ref
  11.4 0.0 copy-done.3
  11.4 2.1 %route.1 = (bf16[72,2048]{1,0:T(8,128)(2,1)S(1)}, f32[72,128]{1,0:T(8,128)S(1)}, f32[72,128]{1,0:T(8,128)S(1)}, bf16[1024,2304]{1,0:T(8,128)(2,1)S(1)}) custom-call(f32[72,2048]{1,0:T(8,128)S(1)} %convert_add_fusion.base_ref, f32[72,2048]{1,0:T(8,128)S(1)} %collective-permute-done.recv_ref, bf16[2048,128]{1,0:T(8,128)(2,1)S(1)} %copy-done.3, ...), custom_call_target="tpu_custom_call" | custom-call | tf_op jit(solution)/shard_map/route/pallas_call | solution.py:260
  13.6 0.0 copy-start
  13.6 0.0 copy-start.1
  13.6 0.0 copy-start.2
  13.6 68.8 %all_to_all.10 = bf16[128,8,2304]{2,1,0:T(8,128)(2,1)S(1)} all-to-all(bf16[128,8,2304]{2,1,0:T(8,128)(2,1)S(1)} %bitcast.9), channel_id=1, replica_groups=mesh['ep'=64,'dp'=2] {'ep','dp'}, dimensions={0} | all-to-all | bytes 9437184 | tf_op jit(solution)/shard_map/all_to_all | solution.py:345
  82.5 0.0 copy-done
  82.5 0.0 copy-done.1
  82.5 0.0 copy-done.2
  82.5 12.1 %expert.1 = bf16[1024,2304]{1,0:T(8,128)(2,1)S(1)} custom-call(bf16[1024,2304]{1,0:T(8,128)(2,1)S(1)} %bitcast.7, bf16[1,2048,768]{2,1,0:T(8,128)(2,1)S(1)} %copy-done, bf16[1,2048,768]{2,1,0:T(8,128)(2,1)S(1)} %copy-done.1, bf16[1,768,2048]{2,1,0:T(8,128)(2,1)S(1)} %copy-done.2), custom_call_target="tpu_custom_call" | custom-call | tf_op jit(solution)/shard_map/expert/pallas_call | solution.py:298
  94.6 63.0 %all_to_all.11 = bf16[128,8,2304]{2,1,0:T(8,128)(2,1)S(1)} all-to-all(bf16[128,8,2304]{2,1,0:T(8,128)(2,1)S(1)} %bitcast.8), channel_id=1, replica_groups=mesh['ep'=64,'dp'=2] {'ep','dp'}, dimensions={0} | all-to-all | bytes 9437184 | tf_op jit(solution)/shard_map/all_to_all | solution.py:345
  157.5 2.0 %combine.1 = bf16[72,2048]{1,0:T(8,128)(2,1)} custom-call(bf16[72,2048]{1,0:T(8,128)(2,1)S(1)} %get-tuple-element.13.hidden_ref, f32[72,128]{1,0:T(8,128)S(1)} %get-tuple-element.14.gate_ref, f32[72,128]{1,0:T(8,128)S(1)} %get-tuple-element.15.rank_ref, bf16[1024,2304]{1,0:T(8,128)(2,1)S(1)} %bitcast.6), custom_call_target="tpu_custom_call" | custom-call | tf_op jit(solution)/shard_map/combine/pallas_call | solution.py:332
  (4 shorter events, 0.0 us)
Async XLA Ops:
  0.0 9.6 %copy-start.5 = (bf16[2048]{0:T(1024)(128)(2,1)S(1)}, bf16[2048]{0:T(1024)(128)(2,1)}, u32[]{:S(2)}) copy-start(bf16[2048]{0:T(1024)(128)(2,1)} %param.24) | copy-start | bytes 12292
  0.0 9.6 %copy-start.6 = (s32[72,8]{0,1:T(8,128)S(1)}, s32[72,8]{0,1:T(8,128)}, u32[]{:S(2)}) copy-start(s32[72,8]{0,1:T(8,128)} %param.25) | copy-start | bytes 6916
  0.0 9.7 %copy-start.7 = (s32[72]{0:T(128)S(1)}, s32[72]{0:T(128)}, u32[]{:S(2)}) copy-start(s32[72]{0:T(128)} %param.26) | copy-start | bytes 868
  0.0 9.8 %copy-start.4 = (bf16[72,2048]{1,0:T(8,128)(2,1)S(1)}, bf16[72,2048]{1,0:T(8,128)(2,1)}, u32[]{:S(2)}) copy-start(bf16[72,2048]{1,0:T(8,128)(2,1)} %param.15) | copy-start | bytes 884740
  0.0 11.4 %copy-start.3 = (bf16[2048,128]{1,0:T(8,128)(2,1)S(1)}, bf16[2048,128]{1,0:T(8,128)(2,1)}, u32[]{:S(2)}) copy-start(bf16[2048,128]{1,0:T(8,128)(2,1)} %router_ref.1) | copy-start | bytes 1572868
  8.2 3.3 %collective-permute-start = (f32[72,2048]{1,0:T(8,128)}, f32[72,2048]{1,0:T(8,128)S(1)}, u32[]{:S(2)}, u32[]{:S(2)}) collective-permute-start(f32[72,2048]{1,0:T(8,128)} %get-tuple-element.12), channel_id=1, source_target_pairs={{0,1},{1,0},{2,3},{3,2},{4,5},{5,4},{6,7},{7,6},{8,9},{9,8},{10,11... | collective-permute-start | bytes 1769480 | tf_op jit(solution)/shard_map/ppermute | solution.py:360
  13.6 68.9 %copy-start = (bf16[1,2048,768]{2,1,0:T(8,128)(2,1)S(1)}, bf16[1,2048,768]{2,1,0:T(8,128)(2,1)}, u32[]{:S(2)}) copy-start(bf16[1,2048,768]{2,1,0:T(8,128)(2,1)} %wg_ref.1) | copy-start | bytes 9437188
  13.6 68.9 %copy-start.1 = (bf16[1,2048,768]{2,1,0:T(8,128)(2,1)S(1)}, bf16[1,2048,768]{2,1,0:T(8,128)(2,1)}, u32[]{:S(2)}) copy-start(bf16[1,2048,768]{2,1,0:T(8,128)(2,1)} %wu_ref.1) | copy-start | bytes 9437188
  13.6 68.9 %copy-start.2 = (bf16[1,768,2048]{2,1,0:T(8,128)(2,1)S(1)}, bf16[1,768,2048]{2,1,0:T(8,128)(2,1)}, u32[]{:S(2)}) copy-start(bf16[1,768,2048]{2,1,0:T(8,128)(2,1)} %wd_ref.1) | copy-start | bytes 9437188

commit v3 on v2

--- a/solution.py
+++ b/solution.py
@@ -191,6 +191,12 @@
 MAIN = 8
 
 
+CHUNK = 320
+GROUPS = 4
+WINDOW = 128
+MARK = 1e-36
+
+
 def spread_last(scr, rows):
     tiles = scr.shape[0]
     for q in range(MAIN):
@@ -244,6 +250,9 @@
     spread = dot(rank.astype(BF16), expander(experts))
     slot = (iota(spread.shape, 1) & (MAIN - 1)).astype(F32) + 1.0
     pick = jnp.where(spread == slot, 1.0, 0.0).astype(BF16)
+    head = normed[:, :HEAD].astype(F32)
+    head = jnp.where((iota(head.shape, 1) == 0) & (head == 0.0), MARK, head).astype(BF16)
+    normed = jnp.concatenate([head, normed[:, HEAD:]], 1)
     block = width // 4
     for n in range(4):
         cs = slice(n * block, (n + 1) * block)
@@ -273,35 +282,100 @@
     )(base, recv, router, gain, ids, live)
 
 
-def expert_kernel(x_ref, wg_ref, wu_ref, wd_ref, y_ref, scr):
+def in_use(rows):
+    used = jnp.where((iota(rows.shape, 1) == 0) & (rows.astype(F32) != 0.0), 1.0, 0.0)
+    return dot_nt(jnp.ones((8, HEAD), BF16), used.astype(BF16))
+
+
+def places(main, last):
+    sources = last.shape[1]
+    grow = expander(sources)
+    slot = iota(main.shape, 1) & (MAIN - 1)
+    upto = main
+    for shift in (1, 2, 4):
+        upto = upto + jnp.where(slot >= shift, pltpu.roll(upto, shift, 1), 0.0)
+    count = dot_nt(main.astype(BF16), grow)
+    held = count + last
+    before = (iota((sources, sources), 0) < iota((sources, sources), 1)).astype(F32).astype(BF16)
+    base = dot(held.astype(BF16), before)
+    high = jnp.floor(base * (1.0 / 64.0))
+    parts = dot(jnp.concatenate([high, base - 64.0 * high], 0).astype(BF16), grow)
+    first = 64.0 * parts[:8] + parts[8:]
+    at_main = jnp.where(main > 0.0, first + upto - 1.0, -1.0)
+    at_last = jnp.where(last > 0.0, base + count, -1.0)
+    return at_main, at_last, base[0:1], jnp.sum(held[0:1]).astype(jnp.int32)
+
+
+def expert_kernel(x_ref, wg_ref, wu_ref, wd_ref, y_ref, scr, x_buf, y_buf):
     wg, wu, wd = wg_ref.at[0], wu_ref.at[0], wd_ref.at[0]
     width = wg.shape[0]
+    count = x_ref.shape[0]
+    sources = count // MAIN
+    last = collect_last(scr, x_ref[:, width:], sources)
+    at_main, at_last, base, total = places(in_use(x_ref[:, :HEAD]), in_use(last[:, :HEAD]))
+    block = width // 4
+    members = sources // GROUPS
+    lane = iota(base.shape, 1)
+    edges = [
+        jnp.sum(jnp.where(lane == j * members, base, 0.0)).astype(jnp.int32) for j in range(GROUPS)
+    ] + [total]
+    starts = [e & ~15 for e in edges[:-1]]
+    fits = total <= CHUNK
+    for j in range(GROUPS):
+        fits = fits & (edges[j + 1] - starts[j] <= WINDOW)
 
     def mlp(x):
         g = dot(x, wg[...])
         u = dot(x, wu[...])
         return dot((g * jax.nn.sigmoid(g) * u).astype(BF16), wd[...])
 
-    count = x_ref.shape[0]
-    last = collect_last(scr, x_ref[:, width:], count // MAIN)
-    y_ref[:, width:] = spread_last(scr, mlp(last))
-    chunk = 256
-
-    @pl.loop(0, count // chunk)
-    def _(i):
-        rows = pl.ds(pl.multiple_of(i * chunk, chunk), chunk)
-        y_ref[rows, :width] = mlp(x_ref[rows, :width]).astype(BF16)
+    def hot(at, rows, start):
+        row = iota((rows, at.shape[1]), 0) + start
+        return jnp.where(at[0:1].astype(jnp.int32) == row, 1.0, 0.0).astype(BF16)
+
+    @pl.when(fits)
+    def _():
+        main, tail = hot(at_main, CHUNK, 0), hot(at_last, CHUNK, 0)
+        for n in range(4):
+            cs = slice(n * block, (n + 1) * block)
+            x_buf[:, cs] = (dot(main, x_ref[:, cs]) + dot(tail, last[:, cs])).astype(BF16)
+        y_buf[:CHUNK, :] = mlp(x_buf[...]).astype(BF16)
+        y_buf[CHUNK:, :] = jnp.zeros((WINDOW, width), BF16)
+        size = members * MAIN
+        for j in range(GROUPS):
+            rows = slice(j * size, (j + 1) * size)
+            near = hot(at_main[:, rows], WINDOW, starts[j])
+            from_ = pl.ds(pl.multiple_of(starts[j], 16), WINDOW)
+            for n in range(4):
+                cs = slice(n * block, (n + 1) * block)
+                y_ref[rows, cs] = dot_tn(near, y_buf[from_, cs]).astype(BF16)
+        y_ref[:, width:] = spread_last(scr, dot_tn(tail, y_buf[:CHUNK, :]))
+
+    @pl.when(jnp.logical_not(fits))
+    def _():
+        y_ref[:, width:] = spread_last(scr, mlp(last))
+        step = 256
+
+        @pl.loop(0, count // step)
+        def _(i):
+            rows = pl.ds(pl.multiple_of(i * step, step), step)
+            y_ref[rows, :width] = mlp(x_ref[rows, :width]).astype(BF16)
 
 
 def expert(x, wg, wu, wd):
     vm = pl.BlockSpec(memory_space=VMEM)
+    width = wg.shape[1]
     return pl.pallas_call(
         expert_kernel,
         name="expert",
         out_shape=jax.ShapeDtypeStruct(x.shape, BF16),
         in_specs=[vm] * 4,
         out_specs=vm,
-        scratch_shapes=[last_scratch(x.shape[0], wg.shape[1])],
+        scratch_shapes=[
+            last_scratch(x.shape[0], width),
+            VMEM((CHUNK, width), BF16),
+            VMEM((CHUNK + WINDOW, width), BF16),
+        ],
         compiler_params=pltpu.CompilerParams(vmem_limit_bytes=LIMIT),
     )(x, wg, wu, wd)
 

time: 160 us -> 155 us (0.969)
  Pallas kernels: 24.3 us -> 19.7 us
    pallas_call x1, Pallas kernels: 12.1 us -> 7.44 us  [expert(): pl.pallas_call(expert_kernel, name='expert', out_shape=jax.ShapeDtypeStru...]
where the time goes in v3:
time: 155 us
  blocking collectives  132 us (85%)
  Pallas kernels  19.7 us (13%)
    all_to_all x2, blocking collectives, exchange(): lax.all_to_all(blocks, ('ep', 'dp'), split_axis=0, concat_axis=0, tiled=T...  132 us
    pallas_call x1, Pallas kernels, attend(): pl.pallas_call(attend_kernel, name='attend', out_shape=(out, out), in_spe...  8.12 us
    pallas_call x1, Pallas kernels, expert(): pl.pallas_call(expert_kernel, name='expert', out_shape=jax.ShapeDtypeStru...  7.44 us
  transfers between devices with their start and end apart: 1, of which 1 were waited for; matrix products, arithmetic and copies ran while one was open for 1% of the time, Pallas kernels for 0%

profile of v3, /device:TPU:1, one launch (start us, length us, event | category | flops | bytes accessed | tf_op | source)
XLA Modules:
  0.0 154.9 jit_solution(16679054217083743615)
XLA Ops:
  0.0 0.0 copy-start.4
  0.0 0.0 copy-start.3
  0.0 8.1 %attend.1 = (f32[72,2048]{1,0:T(8,128)}, f32[72,2048]{1,0:T(8,128)}) custom-call(s32[17]{0:T(128)} %lens_ref.1, s32[1]{0:T(128)} %bitcast.core_ref, bf16[144,2048]{1,0:T(8,128)(2,1)} %q_hbm.1, bf16[144,256]{1,0:T(8,128)(2,1)} %fk_hbm.1, bf16[144,256]{1,0:T(8,128)(2,1)} %fv_hbm.1, bf16[17,256,256]{2,1,0:T(8,128)(2,1)} %ck_hbm.1, ...), custom_call_target="tpu_custom_call" | custom-call | tf_op jit(solution)/shard_map/attend/pallas_call | solution.py:165
  8.2 1.4 collective-permute-start
  9.6 0.0 copy-done.5
  9.6 0.0 copy-done.6
  9.6 0.1 copy.16.ids_ref
  9.7 0.0 copy-done.7
  9.7 0.1 copy.17.live_ref
  9.8 0.0 copy-done.4
  9.8 1.1 convert_add_fusion.base_ref
  10.9 0.5 collective-permute-done.recv_ref
  11.4 0.0 copy-done.3
  11.4 2.1 %route.1 = (bf16[72,2048]{1,0:T(8,128)(2,1)S(1)}, f32[72,128]{1,0:T(8,128)S(1)}, f32[72,128]{1,0:T(8,128)S(1)}, bf16[1024,2304]{1,0:T(8,128)(2,1)S(1)}) custom-call(f32[72,2048]{1,0:T(8,128)S(1)} %convert_add_fusion.base_ref, f32[72,2048]{1,0:T(8,128)S(1)} %collective-permute-done.recv_ref, bf16[2048,128]{1,0:T(8,128)(2,1)S(1)} %copy-done.3, ...), custom_call_target="tpu_custom_call" | custom-call | tf_op jit(solution)/shard_map/route/pallas_call | solution.py:269
  13.6 0.0 copy-start
  13.6 0.0 copy-start.1
  13.6 0.0 copy-start.2
  13.6 68.9 %all_to_all.10 = bf16[128,8,2304]{2,1,0:T(8,128)(2,1)S(1)} all-to-all(bf16[128,8,2304]{2,1,0:T(8,128)(2,1)S(1)} %bitcast.9), channel_id=1, replica_groups=mesh['ep'=64,'dp'=2] {'ep','dp'}, dimensions={0} | all-to-all | bytes 9437184 | tf_op jit(solution)/shard_map/all_to_all | solution.py:419
  82.5 0.0 copy-done
  82.5 0.0 copy-done.1
  82.5 0.0 copy-done.2
  82.5 7.4 %expert.1 = bf16[1024,2304]{1,0:T(8,128)(2,1)S(1)} custom-call(bf16[1024,2304]{1,0:T(8,128)(2,1)S(1)} %bitcast.7, bf16[1,2048,768]{2,1,0:T(8,128)(2,1)S(1)} %copy-done, bf16[1,2048,768]{2,1,0:T(8,128)(2,1)S(1)} %copy-done.1, bf16[1,768,2048]{2,1,0:T(8,128)(2,1)S(1)} %copy-done.2), custom_call_target="tpu_custom_call" | custom-call | tf_op jit(solution)/shard_map/expert/pallas_call | solution.py:368
  89.9 63.0 %all_to_all.11 = bf16[128,8,2304]{2,1,0:T(8,128)(2,1)S(1)} all-to-all(bf16[128,8,2304]{2,1,0:T(8,128)(2,1)S(1)} %bitcast.8), channel_id=1, replica_groups=mesh['ep'=64,'dp'=2] {'ep','dp'}, dimensions={0} | all-to-all | bytes 9437184 | tf_op jit(solution)/shard_map/all_to_all | solution.py:419
  152.9 2.0 %combine.1 = bf16[72,2048]{1,0:T(8,128)(2,1)} custom-call(bf16[72,2048]{1,0:T(8,128)(2,1)S(1)} %get-tuple-element.13.hidden_ref, f32[72,128]{1,0:T(8,128)S(1)} %get-tuple-element.14.gate_ref, f32[72,128]{1,0:T(8,128)S(1)} %get-tuple-element.15.rank_ref, bf16[1024,2304]{1,0:T(8,128)(2,1)S(1)} %bitcast.6), custom_call_target="tpu_custom_call" | custom-call | tf_op jit(solution)/shard_map/combine/pallas_call | solution.py:406
  (4 shorter events, 0.0 us)
Async XLA Ops:
  0.0 9.6 %copy-start.5 = (bf16[2048]{0:T(1024)(128)(2,1)S(1)}, bf16[2048]{0:T(1024)(128)(2,1)}, u32[]{:S(2)}) copy-start(bf16[2048]{0:T(1024)(128)(2,1)} %param.24) | copy-start | bytes 12292
  0.0 9.6 %copy-start.6 = (s32[72,8]{0,1:T(8,128)S(1)}, s32[72,8]{0,1:T(8,128)}, u32[]{:S(2)}) copy-start(s32[72,8]{0,1:T(8,128)} %param.25) | copy-start | bytes 6916
  0.0 9.7 %copy-start.7 = (s32[72]{0:T(128)S(1)}, s32[72]{0:T(128)}, u32[]{:S(2)}) copy-start(s32[72]{0:T(128)} %param.26) | copy-start | bytes 868
  0.0 9.8 %copy-start.4 = (bf16[72,2048]{1,0:T(8,128)(2,1)S(1)}, bf16[72,2048]{1,0:T(8,128)(2,1)}, u32[]{:S(2)}) copy-start(bf16[72,2048]{1,0:T(8,128)(2,1)} %param.15) | copy-start | bytes 884740
  0.0 11.4 %copy-start.3 = (bf16[2048,128]{1,0:T(8,128)(2,1)S(1)}, bf16[2048,128]{1,0:T(8,128)(2,1)}, u32[]{:S(2)}) copy-start(bf16[2048,128]{1,0:T(8,128)(2,1)} %router_ref.1) | copy-start | bytes 1572868
  8.2 3.3 %collective-permute-start = (f32[72,2048]{1,0:T(8,128)}, f32[72,2048]{1,0:T(8,128)S(1)}, u32[]{:S(2)}, u32[]{:S(2)}) collective-permute-start(f32[72,2048]{1,0:T(8,128)} %get-tuple-element.12), channel_id=1, source_target_pairs={{0,1},{1,0},{2,3},{3,2},{4,5},{5,4},{6,7},{7,6},{8,9},{9,8},{10,11... | collective-permute-start | bytes 1769480 | tf_op jit(solution)/shard_map/ppermute | solution.py:434
  13.6 68.9 %copy-start = (bf16[1,2048,768]{2,1,0:T(8,128)(2,1)S(1)}, bf16[1,2048,768]{2,1,0:T(8,128)(2,1)}, u32[]{:S(2)}) copy-start(bf16[1,2048,768]{2,1,0:T(8,128)(2,1)} %wg_ref.1) | copy-start | bytes 9437188
  13.6 68.9 %copy-start.1 = (bf16[1,2048,768]{2,1,0:T(8,128)(2,1)S(1)}, bf16[1,2048,768]{2,1,0:T(8,128)(2,1)}, u32[]{:S(2)}) copy-start(bf16[1,2048,768]{2,1,0:T(8,128)(2,1)} %wu_ref.1) | copy-start | bytes 9437188
  13.6 68.9 %copy-start.2 = (bf16[1,768,2048]{2,1,0:T(8,128)(2,1)S(1)}, bf16[1,768,2048]{2,1,0:T(8,128)(2,1)}, u32[]{:S(2)}) copy-start(bf16[1,768,2048]{2,1,0:T(8,128)(2,1)} %wd_ref.1) | copy-start | bytes 9437188

commit v4 on v3

--- a/solution.py
+++ b/solution.py
@@ -191,7 +191,7 @@
 MAIN = 8
 
 
-CHUNK = 320
+CHUNK = 288
 GROUPS = 4
 WINDOW = 128
 MARK = 1e-36
@@ -224,44 +224,74 @@
     return ((iota(shape, 1) >> 3) == iota(shape, 0)).astype(F32).astype(BF16)
 
 
-def route_kernel(
-    base_ref, recv_ref, router_ref, gain_ref, ids_ref, live_ref,
-    hidden_ref, gate_ref, rank_ref, send_ref, scr,
+def prepare_kernel(
+    res_ref, mine_ref, ids_ref, live_ref, base_ref, chosen_ref, rank_ref, pick_ref, last_ref
 ):
-    rows, width = base_ref.shape
-    experts = router_ref.shape[1]
-    hidden = (base_ref[...] + recv_ref[...]).astype(BF16)
-    hidden_ref[...] = hidden
-    h32 = hidden.astype(F32)
-    mean = jnp.mean(h32 * h32, -1, keepdims=True)
-    normed = (h32 * lax.rsqrt(mean + NORM_EPS) * gain_ref[...].astype(F32)).astype(BF16)
-    logits = dot(normed, router_ref[...])
+    rows = res_ref.shape[0]
+    experts = rank_ref.shape[1]
+    base_ref[...] = res_ref[...].astype(F32) + mine_ref[...]
     lane = iota((rows, experts), 1)
     ids = ids_ref[...]
     chosen = ids[:, 0:1] == lane
     for k in range(1, ids.shape[1]):
         chosen = chosen | (ids[:, k : k + 1] == lane)
-    raised = jnp.where(chosen, jnp.exp(jnp.where(chosen, logits, 0.0)), 0.0)
-    gate_ref[...] = raised / jnp.sum(raised, -1, keepdims=True)
+    chosen_ref[...] = jnp.where(chosen, 1.0, 0.0)
     used = jnp.where(chosen & (live_ref[...] > 0), 1.0, 0.0)
     before = (iota((rows, rows), 0) > iota((rows, rows), 1)).astype(F32).astype(BF16)
     rank = used * (dot(before, used.astype(BF16)) + 1.0)
     rank_ref[...] = rank
     spread = dot(rank.astype(BF16), expander(experts))
     slot = (iota(spread.shape, 1) & (MAIN - 1)).astype(F32) + 1.0
-    pick = jnp.where(spread == slot, 1.0, 0.0).astype(BF16)
+    pick_ref[...] = jnp.where(spread == slot, 1.0, 0.0).astype(BF16)
+    last_ref[...] = jnp.where(rank == MAIN + 1.0, 1.0, 0.0).astype(BF16)
+
+
+def prepare(res, mine, ids, live, experts):
+    rows, width = res.shape
+    vm = pl.BlockSpec(memory_space=VMEM)
+    return pl.pallas_call(
+        prepare_kernel,
+        name="prepare",
+        out_shape=(
+            jax.ShapeDtypeStruct((rows, width), F32),
+            jax.ShapeDtypeStruct((rows, experts), F32),
+            jax.ShapeDtypeStruct((rows, experts), F32),
+            jax.ShapeDtypeStruct((rows, experts * MAIN), BF16),
+            jax.ShapeDtypeStruct((rows, experts), BF16),
+        ),
+        in_specs=[vm] * 4,
+        out_specs=(vm,) * 5,
+        cost_estimate=pl.CostEstimate(flops=2 * rows * width, bytes_accessed=10 * rows * width, transcendentals=0),
+        compiler_params=pltpu.CompilerParams(vmem_limit_bytes=LIMIT),
+    )(res, mine, ids, live)
+
+
+def route_kernel(
+    base_ref, recv_ref, router_ref, gain_ref, chosen_ref, pick_ref, last_ref,
+    hidden_ref, gate_ref, send_ref, scr,
+):
+    width = base_ref.shape[1]
+    hidden = (base_ref[...] + recv_ref[...]).astype(BF16)
+    hidden_ref[...] = hidden
+    h32 = hidden.astype(F32)
+    mean = jnp.mean(h32 * h32, -1, keepdims=True)
+    normed = (h32 * lax.rsqrt(mean + NORM_EPS) * gain_ref[...].astype(F32)).astype(BF16)
     head = normed[:, :HEAD].astype(F32)
     head = jnp.where((iota(head.shape, 1) == 0) & (head == 0.0), MARK, head).astype(BF16)
-    normed = jnp.concatenate([head, normed[:, HEAD:]], 1)
+    marked = jnp.concatenate([head, normed[:, HEAD:]], 1)
+    pick = pick_ref[...]
     block = width // 4
     for n in range(4):
         cs = slice(n * block, (n + 1) * block)
-        send_ref[:, cs] = dot_tn(pick, normed[:, cs]).astype(BF16)
-    last = jnp.where(rank == MAIN + 1.0, 1.0, 0.0).astype(BF16)
-    send_ref[:, width:] = spread_last(scr, dot_tn(last, normed))
-
-
-def route(base, recv, router, gain, ids, live):
+        send_ref[:, cs] = dot_tn(pick, marked[:, cs]).astype(BF16)
+    send_ref[:, width:] = spread_last(scr, dot_tn(last_ref[...], marked))
+    logits = dot(normed, router_ref[...])
+    chosen = chosen_ref[...] > 0.0
+    raised = jnp.where(chosen, jnp.exp(jnp.where(chosen, logits, 0.0)), 0.0)
+    gate_ref[...] = raised / jnp.sum(raised, -1, keepdims=True)
+
+
+def route(base, recv, router, gain, chosen, pick, last):
     rows, width = base.shape
     experts = router.shape[1]
     part = width // MAIN
@@ -272,14 +302,13 @@
         out_shape=(
             jax.ShapeDtypeStruct((rows, width), BF16),
             jax.ShapeDtypeStruct((rows, experts), F32),
-            jax.ShapeDtypeStruct((rows, experts), F32),
             jax.ShapeDtypeStruct((experts * MAIN, width + part), BF16),
         ),
-        in_specs=[vm] * 6,
-        out_specs=(vm,) * 4,
+        in_specs=[vm] * 7,
+        out_specs=(vm,) * 3,
         scratch_shapes=[last_scratch(experts * MAIN, width)],
         compiler_params=pltpu.CompilerParams(vmem_limit_bytes=LIMIT),
-    )(base, recv, router, gain, ids, live)
+    )(base, recv, router, gain, chosen, pick, last)
 
 
 def in_use(rows):
@@ -432,9 +461,11 @@
         request_value_cache, out_proj,
     )
     recv = lax.ppermute(other, "dp", [(0, 1), (1, 0)])
-    hidden, gate, rank, send = route(
-        residual.astype(F32) + mine, recv, router_weight, norm_gain.reshape(1, -1), expert_ids,
-        live_mask.reshape(-1, 1),
+    base, chosen, rank, pick, last = prepare(
+        residual, mine, expert_ids, live_mask.reshape(-1, 1), experts
+    )
+    hidden, gate, send = route(
+        base, recv, router_weight, norm_gain.reshape(1, -1), chosen, pick, last
     )
     back = exchange(expert(exchange(send, experts), w_gate, w_up, w_down), experts)
     return combine(hidden, gate, rank, back)

time: 155 us -> 154 us (level)
  transfers between devices with their start and end apart: 1 -> 1, of which waited for: 1 -> 0; matrix products, arithmetic and copies ran while one was open for 1% -> 0% of each run, Pallas kernels for 0% -> 0%
where the time goes in v4:
time: 154 us
  blocking collectives  132 us (86%)
  Pallas kernels  19.4 us (13%)
    all_to_all x2, blocking collectives, exchange(): lax.all_to_all(blocks, ('ep', 'dp'), split_axis=0, concat_axis=0, tiled=T...  132 us
    pallas_call x1, Pallas kernels, attend(): pl.pallas_call(attend_kernel, name='attend', out_shape=(out, out), in_spe...  8.09 us
    pallas_call x1, Pallas kernels, expert(): pl.pallas_call(expert_kernel, name='expert', out_shape=jax.ShapeDtypeStru...  6.99 us
  transfers between devices with their start and end apart: 1, of which 0 were waited for; matrix products, arithmetic and copies ran while one was open for 0% of the time, Pallas kernels for 0%

profile of v4, /device:TPU:1, one launch (start us, length us, event | category | flops | bytes accessed | tf_op | source)
XLA Modules:
  0.0 154.1 jit_solution(13283882638087999796)
XLA Ops:
  0.0 0.0 copy-start.7
  0.0 0.0 copy-start.4
  0.0 8.1 %attend.1 = (f32[72,2048]{1,0:T(8,128)}, f32[72,2048]{1,0:T(8,128)}) custom-call(s32[17]{0:T(128)} %lens_ref.1, s32[1]{0:T(128)} %bitcast.core_ref, bf16[144,2048]{1,0:T(8,128)(2,1)} %q_hbm.1, bf16[144,256]{1,0:T(8,128)(2,1)} %fk_hbm.1, bf16[144,256]{1,0:T(8,128)(2,1)} %fv_hbm.1, bf16[17,256,256]{2,1,0:T(8,128)(2,1)} %ck_hbm.1, ...), custom_call_target="tpu_custom_call" | custom-call | tf_op jit(solution)/shard_map/attend/pallas_call | solution.py:165
  8.1 1.4 collective-permute-start
  9.6 0.0 copy-done.6
  9.6 0.1 copy.16.ids_ref
  9.7 0.0 copy-done.8
  9.7 0.1 copy.17.live_ref
  9.8 0.0 copy-done.5
  9.8 1.1 copy-done.3
  10.8 0.5 prepare.1
  11.3 0.0 copy-done.7
  11.4 0.0 collective-permute-done.recv_ref
  11.4 0.0 copy-done.4
  11.4 1.8 %route.1 = (bf16[72,2048]{1,0:T(8,128)(2,1)S(1)}, f32[72,128]{1,0:T(8,128)S(1)}, bf16[1024,2304]{1,0:T(8,128)(2,1)S(1)}) custom-call(f32[72,2048]{1,0:T(8,128)S(1)} %get-tuple-element.16.base_ref, f32[72,2048]{1,0:T(8,128)S(1)} %collective-permute-done.recv_ref, bf16[2048,128]{1,0:T(8,128)(2,1)S(1)} %copy-done.4, bf16[1,2048]{1,0:T(2,128)(2,1)S(1)} %reshape.23.gain_ref, ...), custom_call_target="tpu_custom_call" | custom-call | tf_op jit(solution)/shard_map/route/pallas_call | solution.py:299
  13.2 0.0 copy-start
  13.2 0.0 copy-start.1
  13.2 0.0 copy-start.2
  13.2 68.9 %all_to_all.10 = bf16[128,8,2304]{2,1,0:T(8,128)(2,1)S(1)} all-to-all(bf16[128,8,2304]{2,1,0:T(8,128)(2,1)S(1)} %bitcast.9), channel_id=1, replica_groups=mesh['ep'=64,'dp'=2] {'ep','dp'}, dimensions={0} | all-to-all | bytes 9437184 | tf_op jit(solution)/shard_map/all_to_all | solution.py:448
  82.1 0.0 copy-done
  82.1 0.0 copy-done.2
  82.1 7.0 %expert.1 = bf16[1024,2304]{1,0:T(8,128)(2,1)S(1)} custom-call(bf16[1024,2304]{1,0:T(8,128)(2,1)S(1)} %bitcast.7, bf16[1,2048,768]{2,1,0:T(8,128)(2,1)S(1)} %copy-done, bf16[1,2048,768]{2,1,0:T(8,128)(2,1)S(1)} %copy-done.1, bf16[1,768,2048]{2,1,0:T(8,128)(2,1)S(1)} %copy-done.2), custom_call_target="tpu_custom_call" | custom-call | tf_op jit(solution)/shard_map/expert/pallas_call | solution.py:397
  89.1 63.0 %all_to_all.11 = bf16[128,8,2304]{2,1,0:T(8,128)(2,1)S(1)} all-to-all(bf16[128,8,2304]{2,1,0:T(8,128)(2,1)S(1)} %bitcast.8), channel_id=1, replica_groups=mesh['ep'=64,'dp'=2] {'ep','dp'}, dimensions={0} | all-to-all | bytes 9437184 | tf_op jit(solution)/shard_map/all_to_all | solution.py:448
  152.1 2.0 %combine.1 = bf16[72,2048]{1,0:T(8,128)(2,1)} custom-call(bf16[72,2048]{1,0:T(8,128)(2,1)S(1)} %get-tuple-element.21.hidden_ref, f32[72,128]{1,0:T(8,128)S(1)} %get-tuple-element.22.gate_ref, f32[72,128]{1,0:T(8,128)S(1)} %get-tuple-element.23.rank_ref, bf16[1024,2304]{1,0:T(8,128)(2,1)S(1)} %bitcast.6), custom_call_target="tpu_custom_call" | custom-call | tf_op jit(solution)/shard_map/combine/pallas_call | solution.py:435
  (6 shorter events, 0.0 us)
Async XLA Ops:
  0.0 9.6 %copy-start.6 = (s32[72,8]{0,1:T(8,128)S(1)}, s32[72,8]{0,1:T(8,128)}, u32[]{:S(2)}) copy-start(s32[72,8]{0,1:T(8,128)} %param.25) | copy-start | bytes 6916
  0.0 9.7 %copy-start.8 = (s32[72]{0:T(128)S(1)}, s32[72]{0:T(128)}, u32[]{:S(2)}) copy-start(s32[72]{0:T(128)} %param.26) | copy-start | bytes 868
  0.0 9.8 %copy-start.5 = (bf16[72,2048]{1,0:T(8,128)(2,1)S(1)}, bf16[72,2048]{1,0:T(8,128)(2,1)}, u32[]{:S(2)}) copy-start(bf16[72,2048]{1,0:T(8,128)(2,1)} %res_ref.1) | copy-start | bytes 884740
  0.0 11.3 %copy-start.7 = (bf16[2048]{0:T(1024)(128)(2,1)S(1)}, bf16[2048]{0:T(1024)(128)(2,1)}, u32[]{:S(2)}) copy-start(bf16[2048]{0:T(1024)(128)(2,1)} %param.24) | copy-start | bytes 12292
  0.0 11.4 %copy-start.4 = (bf16[2048,128]{1,0:T(8,128)(2,1)S(1)}, bf16[2048,128]{1,0:T(8,128)(2,1)}, u32[]{:S(2)}) copy-start(bf16[2048,128]{1,0:T(8,128)(2,1)} %router_ref.1) | copy-start | bytes 1572868
  8.1 3.3 %collective-permute-start = (f32[72,2048]{1,0:T(8,128)}, f32[72,2048]{1,0:T(8,128)S(1)}, u32[]{:S(2)}, u32[]{:S(2)}) collective-permute-start(f32[72,2048]{1,0:T(8,128)} %get-tuple-element.17), channel_id=1, source_target_pairs={{0,1},{1,0},{2,3},{3,2},{4,5},{5,4},{6,7},{7,6},{8,9},{9,8},{10,11... | collective-permute-start | bytes 1769480 | tf_op jit(solution)/shard_map/ppermute | solution.py:463
  9.8 1.1 copy-start.3
  13.2 68.9 %copy-start = (bf16[1,2048,768]{2,1,0:T(8,128)(2,1)S(1)}, bf16[1,2048,768]{2,1,0:T(8,128)(2,1)}, u32[]{:S(2)}) copy-start(bf16[1,2048,768]{2,1,0:T(8,128)(2,1)} %wg_ref.1) | copy-start | bytes 9437188
  13.2 68.9 %copy-start.1 = (bf16[1,2048,768]{2,1,0:T(8,128)(2,1)S(1)}, bf16[1,2048,768]{2,1,0:T(8,128)(2,1)}, u32[]{:S(2)}) copy-start(bf16[1,2048,768]{2,1,0:T(8,128)(2,1)} %wu_ref.1) | copy-start | bytes 9437188
  13.2 68.9 %copy-start.2 = (bf16[1,768,2048]{2,1,0:T(8,128)(2,1)S(1)}, bf16[1,768,2048]{2,1,0:T(8,128)(2,1)}, u32[]{:S(2)}) copy-start(bf16[1,768,2048]{2,1,0:T(8,128)(2,1)} %wd_ref.1) | copy-start | bytes 9437188

commit v5 on v4

--- a/solution.py
+++ b/solution.py
@@ -14,7 +14,7 @@
 BF16 = jnp.bfloat16
 VMEM = pltpu.VMEM
 LIMIT = 30 * 1024 * 1024
-FULL = 60 * 1024 * 1024
+FULL = 52 * 1024 * 1024
 
 
 def dot(a, b):
@@ -162,6 +162,7 @@
     sm = pl.BlockSpec(memory_space=pltpu.SMEM)
     hb = pl.BlockSpec(memory_space=pl.ANY)
     out = jax.ShapeDtypeStruct((own, wo.shape[1]), F32)
+    pinned = [pltpu.with_memory_space_constraint(a, pltpu.HBM) for a in (lens, q, fk, fv, ck, cv, wo)]
     return pl.pallas_call(
         attend_kernel,
         name="attend",
@@ -185,7 +186,7 @@
             pltpu.SemaphoreType.DMA((6, 4)),
         ],
         compiler_params=pltpu.CompilerParams(vmem_limit_bytes=FULL),
-    )(lens, core, q, fk, fv, ck, cv, wo)
+    )(pinned[0], core, *pinned[1:])
 
 
 MAIN = 8

time: 154 us -> 153 us (level)
  transfers between devices with their start and end apart: 1 -> 1, of which waited for: 0 -> 1; matrix products, arithmetic and copies ran while one was open for 0% -> 0% of each run, Pallas kernels for 0% -> 0%
where the time goes in v5:
time: 153 us
  blocking collectives  132 us (86%)
  Pallas kernels  18.9 us (12%)
    all_to_all x2, blocking collectives, exchange(): lax.all_to_all(blocks, ('ep', 'dp'), split_axis=0, concat_axis=0, tiled=T...  132 us
    pallas_call x1, Pallas kernels, attend(): pl.pallas_call(attend_kernel, name='attend', out_shape=(out, out), in_spe...  7.58 us
    pallas_call x1, Pallas kernels, expert(): pl.pallas_call(expert_kernel, name='expert', out_shape=jax.ShapeDtypeStru...  6.99 us
  transfers between devices with their start and end apart: 1, of which 1 were waited for; matrix products, arithmetic and copies ran while one was open for 0% of the time, Pallas kernels for 0%

profile of v5, /device:TPU:1, one launch (start us, length us, event | category | flops | bytes accessed | tf_op | source)
XLA Modules:
  0.0 153.3 jit_solution(4180983181851948463)
XLA Ops:
  0.0 0.0 copy-start.6
  0.0 0.0 copy-start.3
  0.0 7.6 %attend.1 = (f32[72,2048]{1,0:T(8,128)S(1)}, f32[72,2048]{1,0:T(8,128)S(1)}) custom-call(s32[17]{0:T(128)} %lens_ref.1, s32[1]{0:T(128)} %bitcast.core_ref, bf16[144,2048]{1,0:T(8,128)(2,1)} %q_hbm.1, bf16[144,256]{1,0:T(8,128)(2,1)} %fk_hbm.1, bf16[144,256]{1,0:T(8,128)(2,1)} %fv_hbm.1, bf16[17,256,256]{2,1,0:T(8,128)(2,1)} %ck_hbm.1, ...), custom_call_target="tpu_custom_call" | custom-call | tf_op jit(solution)/shard_map/attend/pallas_call | solution.py:166
  7.6 1.4 collective-permute-start
  9.1 0.0 copy-done.5
  9.1 0.1 copy.16.ids_ref
  9.1 0.0 copy-done.7
  9.1 0.1 copy.17.live_ref
  9.2 0.0 copy-done.4
  9.2 0.5 prepare.1
  9.8 0.0 copy-done.6
  9.8 0.9 collective-permute-done.recv_ref
  10.7 0.0 copy-done.3
  10.7 1.8 %route.1 = (bf16[72,2048]{1,0:T(8,128)(2,1)S(1)}, f32[72,128]{1,0:T(8,128)S(1)}, bf16[1024,2304]{1,0:T(8,128)(2,1)S(1)}) custom-call(f32[72,2048]{1,0:T(8,128)S(1)} %get-tuple-element.16.base_ref, f32[72,2048]{1,0:T(8,128)S(1)} %collective-permute-done.recv_ref, bf16[2048,128]{1,0:T(8,128)(2,1)S(1)} %copy-done.3, bf16[1,2048]{1,0:T(2,128)(2,1)S(1)} %reshape.23.gain_ref, ...), custom_call_target="tpu_custom_call" | custom-call | tf_op jit(solution)/shard_map/route/pallas_call | solution.py:300
  12.5 0.0 copy-start
  12.5 0.0 copy-start.1
  12.5 0.0 copy-start.2
  12.5 68.8 %all_to_all.10 = bf16[128,8,2304]{2,1,0:T(8,128)(2,1)S(1)} all-to-all(bf16[128,8,2304]{2,1,0:T(8,128)(2,1)S(1)} %bitcast.9), channel_id=1, replica_groups=mesh['ep'=64,'dp'=2] {'ep','dp'}, dimensions={0} | all-to-all | bytes 9437184 | tf_op jit(solution)/shard_map/all_to_all | solution.py:449
  81.4 0.0 copy-done
  81.4 0.0 copy-done.1
  81.4 0.0 copy-done.2
  81.4 7.0 %expert.1 = bf16[1024,2304]{1,0:T(8,128)(2,1)S(1)} custom-call(bf16[1024,2304]{1,0:T(8,128)(2,1)S(1)} %bitcast.7, bf16[1,2048,768]{2,1,0:T(8,128)(2,1)S(1)} %copy-done, bf16[1,2048,768]{2,1,0:T(8,128)(2,1)S(1)} %copy-done.1, bf16[1,768,2048]{2,1,0:T(8,128)(2,1)S(1)} %copy-done.2), custom_call_target="tpu_custom_call" | custom-call | tf_op jit(solution)/shard_map/expert/pallas_call | solution.py:398
  88.4 63.0 %all_to_all.11 = bf16[128,8,2304]{2,1,0:T(8,128)(2,1)S(1)} all-to-all(bf16[128,8,2304]{2,1,0:T(8,128)(2,1)S(1)} %bitcast.8), channel_id=1, replica_groups=mesh['ep'=64,'dp'=2] {'ep','dp'}, dimensions={0} | all-to-all | bytes 9437184 | tf_op jit(solution)/shard_map/all_to_all | solution.py:449
  151.3 2.0 %combine.1 = bf16[72,2048]{1,0:T(8,128)(2,1)} custom-call(bf16[72,2048]{1,0:T(8,128)(2,1)S(1)} %get-tuple-element.21.hidden_ref, f32[72,128]{1,0:T(8,128)S(1)} %get-tuple-element.22.gate_ref, f32[72,128]{1,0:T(8,128)S(1)} %get-tuple-element.23.rank_ref, bf16[1024,2304]{1,0:T(8,128)(2,1)S(1)} %bitcast.6), custom_call_target="tpu_custom_call" | custom-call | tf_op jit(solution)/shard_map/combine/pallas_call | solution.py:436
  (4 shorter events, 0.0 us)
Async XLA Ops:
  0.0 9.1 %copy-start.5 = (s32[72,8]{0,1:T(8,128)S(1)}, s32[72,8]{0,1:T(8,128)}, u32[]{:S(2)}) copy-start(s32[72,8]{0,1:T(8,128)} %param.25) | copy-start | bytes 6916
  0.0 9.1 %copy-start.7 = (s32[72]{0:T(128)S(1)}, s32[72]{0:T(128)}, u32[]{:S(2)}) copy-start(s32[72]{0:T(128)} %param.26) | copy-start | bytes 868
  0.0 9.2 %copy-start.4 = (bf16[72,2048]{1,0:T(8,128)(2,1)S(1)}, bf16[72,2048]{1,0:T(8,128)(2,1)}, u32[]{:S(2)}) copy-start(bf16[72,2048]{1,0:T(8,128)(2,1)} %res_ref.1) | copy-start | bytes 884740
  0.0 9.8 %copy-start.6 = (bf16[2048]{0:T(1024)(128)(2,1)S(1)}, bf16[2048]{0:T(1024)(128)(2,1)}, u32[]{:S(2)}) copy-start(bf16[2048]{0:T(1024)(128)(2,1)} %param.24) | copy-start | bytes 12292
  0.0 10.7 %copy-start.3 = (bf16[2048,128]{1,0:T(8,128)(2,1)S(1)}, bf16[2048,128]{1,0:T(8,128)(2,1)}, u32[]{:S(2)}) copy-start(bf16[2048,128]{1,0:T(8,128)(2,1)} %router_ref.1) | copy-start | bytes 1572868
  7.6 3.1 %collective-permute-start = (f32[72,2048]{1,0:T(8,128)S(1)}, f32[72,2048]{1,0:T(8,128)S(1)}, u32[]{:S(2)}, u32[]{:S(2)}) collective-permute-start(f32[72,2048]{1,0:T(8,128)S(1)} %get-tuple-element.17), channel_id=1, source_target_pairs={{0,1},{1,0},{2,3},{3,2},{4,5},{5,4},{6,7},{7,6},{8,9},{9,8},{10,11... | collective-permute-start | bytes 1769480 | tf_op jit(solution)/shard_map/ppermute | solution.py:464
  12.5 68.9 %copy-start = (bf16[1,2048,768]{2,1,0:T(8,128)(2,1)S(1)}, bf16[1,2048,768]{2,1,0:T(8,128)(2,1)}, u32[]{:S(2)}) copy-start(bf16[1,2048,768]{2,1,0:T(8,128)(2,1)} %wg_ref.1) | copy-start | bytes 9437188
  12.5 68.9 %copy-start.1 = (bf16[1,2048,768]{2,1,0:T(8,128)(2,1)S(1)}, bf16[1,2048,768]{2,1,0:T(8,128)(2,1)}, u32[]{:S(2)}) copy-start(bf16[1,2048,768]{2,1,0:T(8,128)(2,1)} %wu_ref.1) | copy-start | bytes 9437188
  12.5 68.9 %copy-start.2 = (bf16[1,768,2048]{2,1,0:T(8,128)(2,1)S(1)}, bf16[1,768,2048]{2,1,0:T(8,128)(2,1)}, u32[]{:S(2)}) copy-start(bf16[1,768,2048]{2,1,0:T(8,128)(2,1)} %wd_ref.1) | copy-start | bytes 9437188

commit v6 on v5

--- a/solution.py
+++ b/solution.py
@@ -59,7 +59,7 @@
     for i, (lo, hi) in enumerate(cuts):
         copies.append(pltpu.make_async_copy(ck_hbm.at[pl.ds(lo, hi - lo)], k_buf.at[pl.ds(lo, hi - lo)], sem.at[0, i]))
         copies.append(pltpu.make_async_copy(cv_hbm.at[pl.ds(lo, hi - lo)], v_buf.at[pl.ds(lo, hi - lo)], sem.at[1, i]))
-    pieces = 4
+    pieces = 8
     step = wo_buf.shape[1] // pieces
     weights = [
         pltpu.make_async_copy(wo_hbm.at[:, pl.ds(i * step, step)], wo_buf.at[:, pl.ds(i * step, step)], sem.at[2, i])
@@ -183,7 +183,7 @@
             VMEM((pairs, HEAD), F32),
             VMEM((pairs, slots), F32),
             VMEM((pairs, HEAD), F32),
-            pltpu.SemaphoreType.DMA((6, 4)),
+            pltpu.SemaphoreType.DMA((6, 8)),
         ],
         compiler_params=pltpu.CompilerParams(vmem_limit_bytes=FULL),
     )(pinned[0], core, *pinned[1:])
@@ -226,10 +226,13 @@
 
 
 def prepare_kernel(
-    res_ref, mine_ref, ids_ref, live_ref, base_ref, chosen_ref, rank_ref, pick_ref, last_ref
+    res_ref, mine_ref, ids_ref, live_ref, router_hbm,
+    base_ref, chosen_ref, rank_ref, pick_ref, last_ref, router_ref, sem,
 ):
     rows = res_ref.shape[0]
     experts = rank_ref.shape[1]
+    load = pltpu.make_async_copy(router_hbm, router_ref, sem)
+    load.start()
     base_ref[...] = res_ref[...].astype(F32) + mine_ref[...]
     lane = iota((rows, experts), 1)
     ids = ids_ref[...]
@@ -245,10 +248,13 @@
     slot = (iota(spread.shape, 1) & (MAIN - 1)).astype(F32) + 1.0
     pick_ref[...] = jnp.where(spread == slot, 1.0, 0.0).astype(BF16)
     last_ref[...] = jnp.where(rank == MAIN + 1.0, 1.0, 0.0).astype(BF16)
-
-
-def prepare(res, mine, ids, live, experts):
+    load.wait()
+
+
+def prepare(res, mine, ids, live, router):
     rows, width = res.shape
+    experts = router.shape[1]
+    res, router = [pltpu.with_memory_space_constraint(a, pltpu.HBM) for a in (res, router)]
     vm = pl.BlockSpec(memory_space=VMEM)
     return pl.pallas_call(
         prepare_kernel,
@@ -259,12 +265,14 @@
             jax.ShapeDtypeStruct((rows, experts), F32),
             jax.ShapeDtypeStruct((rows, experts * MAIN), BF16),
             jax.ShapeDtypeStruct((rows, experts), BF16),
+            jax.ShapeDtypeStruct(router.shape, BF16),
         ),
-        in_specs=[vm] * 4,
-        out_specs=(vm,) * 5,
+        in_specs=[vm] * 4 + [pl.BlockSpec(memory_space=pl.ANY)],
+        out_specs=(vm,) * 6,
+        scratch_shapes=[pltpu.SemaphoreType.DMA],
         cost_estimate=pl.CostEstimate(flops=2 * rows * width, bytes_accessed=10 * rows * width, transcendentals=0),
         compiler_params=pltpu.CompilerParams(vmem_limit_bytes=LIMIT),
-    )(res, mine, ids, live)
+    )(res, mine, ids, live, router)
 
 
 def route_kernel(
@@ -462,11 +470,11 @@
         request_value_cache, out_proj,
     )
     recv = lax.ppermute(other, "dp", [(0, 1), (1, 0)])
-    base, chosen, rank, pick, last = prepare(
-        residual, mine, expert_ids, live_mask.reshape(-1, 1), experts
+    base, chosen, rank, pick, last, router_here = prepare(
+        residual, mine, expert_ids, live_mask.reshape(-1, 1), router_weight
     )
     hidden, gate, send = route(
-        base, recv, router_weight, norm_gain.reshape(1, -1), chosen, pick, last
+        base, recv, router_here, norm_gain.reshape(1, -1), chosen, pick, last
     )
     back = exchange(expert(exchange(send, experts), w_gate, w_up, w_down), experts)
     return combine(hidden, gate, rank, back)

time: 153 us -> 156 us (1.020)
  Pallas kernels: 18.9 us -> 22.3 us
    pallas_call x1, Pallas kernels: 7.58 us -> 9.49 us  [attend(): pl.pallas_call(attend_kernel, name='attend', out_shape=(out, out), in_spe...]
  transfers between devices with their start and end apart: 1 -> 1, of which waited for: 1 -> 0; matrix products, arithmetic and copies ran while one was open for 0% -> 0% of each run, Pallas kernels for 0% -> 1%
where the time goes in v6:
time: 156 us
  blocking collectives  132 us (85%)
  Pallas kernels  22.3 us (14%)
    all_to_all x2, blocking collectives, exchange(): lax.all_to_all(blocks, ('ep', 'dp'), split_axis=0, concat_axis=0, tiled=T...  132 us
    pallas_call x1, Pallas kernels, attend(): pl.pallas_call(attend_kernel, name='attend', out_shape=(out, out), in_spe...  9.49 us
    pallas_call x1, Pallas kernels, expert(): pl.pallas_call(expert_kernel, name='expert', out_shape=jax.ShapeDtypeStru...  6.99 us
  transfers between devices with their start and end apart: 1, of which 0 were waited for; matrix products, arithmetic and copies ran while one was open for 0% of the time, Pallas kernels for 1%

profile of v6, /device:TPU:1, one launch (start us, length us, event | category | flops | bytes accessed | tf_op | source)
XLA Modules:
  0.0 155.6 jit_solution(17031352718978737388)
XLA Ops:
  0.0 0.0 copy-start.3
  0.0 0.0 copy-start.5
  0.0 0.0 copy-start.4
  0.0 9.5 %attend.1 = (f32[72,2048]{1,0:T(8,128)S(1)}, f32[72,2048]{1,0:T(8,128)S(1)}) custom-call(s32[17]{0:T(128)} %lens_ref.1, s32[1]{0:T(128)} %bitcast.core_ref, bf16[144,2048]{1,0:T(8,128)(2,1)} %q_hbm.1, bf16[144,256]{1,0:T(8,128)(2,1)} %fk_hbm.1, bf16[144,256]{1,0:T(8,128)(2,1)} %fv_hbm.1, bf16[17,256,256]{2,1,0:T(8,128)(2,1)} %ck_hbm.1, ...), custom_call_target="tpu_custom_call" | custom-call | tf_op jit(solution)/shard_map/attend/pallas_call | solution.py:166
  9.5 1.5 collective-permute-start
  11.0 0.0 copy-done.3
  11.0 0.1 copy.16.ids_ref
  11.1 0.0 copy-done.5
  11.1 0.1 copy.17.live_ref
  11.2 2.0 %prepare.1 = (f32[72,2048]{1,0:T(8,128)S(1)}, f32[72,128]{1,0:T(8,128)S(1)}, f32[72,128]{1,0:T(8,128)S(1)}, bf16[72,1024]{1,0:T(8,128)(2,1)S(1)}, bf16[72,128]{1...) custom-call(bf16[72,2048]{1,0:T(8,128)(2,1)} %res_ref.1, f32[72,2048]{1,0:T(8,128)S(1)} %get-tuple-element.16.mine_ref, ...), custom_call_target="tpu_custom_call" | custom-call | flops 294912 | bytes 1474560 | tf_op jit(solution)/shard_map/prepare/pallas_call | solution.py:259
  13.2 0.0 copy-done.4
  13.2 0.0 collective-permute-done.recv_ref
  13.2 1.8 %route.1 = (bf16[72,2048]{1,0:T(8,128)(2,1)S(1)}, f32[72,128]{1,0:T(8,128)S(1)}, bf16[1024,2304]{1,0:T(8,128)(2,1)S(1)}) custom-call(f32[72,2048]{1,0:T(8,128)S(1)} %get-tuple-element.17.base_ref, f32[72,2048]{1,0:T(8,128)S(1)} %collective-permute-done.recv_ref, bf16[2048,128]{1,0:T(8,128)(2,1)S(1)} %get-tuple-element.19.router_ref, ...), custom_call_target="tpu_custom_call" | custom-call | tf_op jit(solution)/shard_map/route/pallas_call | solution.py:308
  15.0 0.0 copy-start
  15.0 0.0 copy-start.1
  15.0 0.0 copy-start.2
  15.0 68.6 %all_to_all.10 = bf16[128,8,2304]{2,1,0:T(8,128)(2,1)S(1)} all-to-all(bf16[128,8,2304]{2,1,0:T(8,128)(2,1)S(1)} %bitcast.9), channel_id=1, replica_groups=mesh['ep'=64,'dp'=2] {'ep','dp'}, dimensions={0} | all-to-all | bytes 9437184 | tf_op jit(solution)/shard_map/all_to_all | solution.py:457
  83.6 0.0 copy-done
  83.6 0.0 copy-done.1
  83.6 0.0 copy-done.2
  83.6 7.0 %expert.1 = bf16[1024,2304]{1,0:T(8,128)(2,1)S(1)} custom-call(bf16[1024,2304]{1,0:T(8,128)(2,1)S(1)} %bitcast.7, bf16[1,2048,768]{2,1,0:T(8,128)(2,1)S(1)} %copy-done, bf16[1,2048,768]{2,1,0:T(8,128)(2,1)S(1)} %copy-done.1, bf16[1,768,2048]{2,1,0:T(8,128)(2,1)S(1)} %copy-done.2), custom_call_target="tpu_custom_call" | custom-call | tf_op jit(solution)/shard_map/expert/pallas_call | solution.py:406
  90.6 63.0 %all_to_all.11 = bf16[128,8,2304]{2,1,0:T(8,128)(2,1)S(1)} all-to-all(bf16[128,8,2304]{2,1,0:T(8,128)(2,1)S(1)} %bitcast.8), channel_id=1, replica_groups=mesh['ep'=64,'dp'=2] {'ep','dp'}, dimensions={0} | all-to-all | bytes 9437184 | tf_op jit(solution)/shard_map/all_to_all | solution.py:457
  153.6 2.0 %combine.1 = bf16[72,2048]{1,0:T(8,128)(2,1)} custom-call(bf16[72,2048]{1,0:T(8,128)(2,1)S(1)} %get-tuple-element.23.hidden_ref, f32[72,128]{1,0:T(8,128)S(1)} %get-tuple-element.24.gate_ref, f32[72,128]{1,0:T(8,128)S(1)} %get-tuple-element.25.rank_ref, bf16[1024,2304]{1,0:T(8,128)(2,1)S(1)} %bitcast.6), custom_call_target="tpu_custom_call" | custom-call | tf_op jit(solution)/shard_map/combine/pallas_call | solution.py:444
  (1 shorter events, 0.0 us)
Async XLA Ops:
  0.0 11.0 %copy-start.3 = (s32[72,8]{0,1:T(8,128)S(1)}, s32[72,8]{0,1:T(8,128)}, u32[]{:S(2)}) copy-start(s32[72,8]{0,1:T(8,128)} %param.25) | copy-start | bytes 6916
  0.0 11.1 %copy-start.5 = (s32[72]{0:T(128)S(1)}, s32[72]{0:T(128)}, u32[]{:S(2)}) copy-start(s32[72]{0:T(128)} %param.26) | copy-start | bytes 868
  0.0 13.2 %copy-start.4 = (bf16[2048]{0:T(1024)(128)(2,1)S(1)}, bf16[2048]{0:T(1024)(128)(2,1)}, u32[]{:S(2)}) copy-start(bf16[2048]{0:T(1024)(128)(2,1)} %param.24) | copy-start | bytes 12292
  9.5 3.7 %collective-permute-start = (f32[72,2048]{1,0:T(8,128)S(1)}, f32[72,2048]{1,0:T(8,128)S(1)}, u32[]{:S(2)}, u32[]{:S(2)}) collective-permute-start(f32[72,2048]{1,0:T(8,128)S(1)} %get-tuple-element.18), channel_id=1, source_target_pairs={{0,1},{1,0},{2,3},{3,2},{4,5},{5,4},{6,7},{7,6},{8,9},{9,8},{10,11... | collective-permute-start | bytes 1769480 | tf_op jit(solution)/shard_map/ppermute | solution.py:472
  15.0 68.6 %copy-start = (bf16[1,2048,768]{2,1,0:T(8,128)(2,1)S(1)}, bf16[1,2048,768]{2,1,0:T(8,128)(2,1)}, u32[]{:S(2)}) copy-start(bf16[1,2048,768]{2,1,0:T(8,128)(2,1)} %wg_ref.1) | copy-start | bytes 9437188
  15.0 68.6 %copy-start.1 = (bf16[1,2048,768]{2,1,0:T(8,128)(2,1)S(1)}, bf16[1,2048,768]{2,1,0:T(8,128)(2,1)}, u32[]{:S(2)}) copy-start(bf16[1,2048,768]{2,1,0:T(8,128)(2,1)} %wu_ref.1) | copy-start | bytes 9437188
  15.0 68.6 %copy-start.2 = (bf16[1,768,2048]{2,1,0:T(8,128)(2,1)S(1)}, bf16[1,768,2048]{2,1,0:T(8,128)(2,1)}, u32[]{:S(2)}) copy-start(bf16[1,768,2048]{2,1,0:T(8,128)(2,1)} %wd_ref.1) | copy-start | bytes 9437188
